TPU v7x, 32 devices: a whole 2x2x4 slice. The times are simulated.
32 devices in a mesh: grp: 2 (over y), col: 4 (over z), row: 2 (over x), limb: 2 (over core).
Axes of the slice: x: 2, y: 2, z: 4, core: 2. Of those that a mesh axis runs over, the one named last changes fastest.
Arguments:
- database: bfloat16 [8192, 8192], P(('grp', 'row'), 'col'), parts along dimension 0, may hold values from -128 to 127, as said below
- lwe_matrix: bfloat16 [8192, 2, 512], P('col', 'limb'), may hold values from -0.0008544922 to 0.0008544922
- secret_ct: float32 [2, 2, 2, 512, 4096], P(None, None, 'limb', 'col', 'row'), may hold values from -6 to 6
Outputs:
- encrypted_product: float32 [4, 2, 4096], P('grp', None, 'row'), parts along dimension 0
There are 2 independent parts, one for each index of `grp`. A program takes and returns all parts, laid end to end along the dimension named above; an argument that names none is the same for every part. Nothing has to cross between parts.
Inputs may be any that keep to these rules, and one draw needn't show every extreme that they name: `database`: whole numbers.
All inputs are finite; a program needn't handle non-finite values.
Results may differ from a plain program's by a relative error of at most 0.0003.
Values sent between devices are 32-bit elements; how exact they have to be, the bound alone decides.
A program may use at most 64 MiB of HBM per device.

v0:
```python
import functools
import math

import jax
import jax.numpy as jnp
import numpy as np
from jax import lax
from jax.experimental import pallas as pl
from jax.experimental.pallas import tpu as pltpu
from jax.sharding import PartitionSpec as P

CHUNKS = 4
MESH = pl.DeviceIdType.MESH


def hint_kernel(cols, rows, a_ref, d_hbm, out_ref, d_buf, part, from_left, from_right,
                d_sem, send_sem, recv_sem, row_send, row_recv):
    me = lax.axis_index("col")
    row = lax.axis_index("row")
    own, width = part.shape[2:]
    has_left, has_right = me > 0, me < cols - 1
    loads = [
        pltpu.make_async_copy(d_hbm.at[pl.ds(k * width, width)], d_buf.at[k], d_sem.at[k])
        for k in range(CHUNKS)
    ]
    for load in loads:
        load.start()
    barrier = pltpu.get_barrier_semaphore()
    for there, side in ((has_left, -1), (has_right, 1)):
        @pl.when(there)
        def _():
            pl.semaphore_signal(barrier, inc=1, device_id={"col": me + side}, device_id_type=MESH)
    for step in range(1, rows):
        pl.semaphore_signal(
            barrier, inc=1, device_id={"row": lax.rem(row + step, rows)}, device_id_type=MESH
        )
    inner = has_left & has_right

    @pl.when(inner)
    def _():
        pl.semaphore_wait(barrier, rows + 1)

    @pl.when(jnp.logical_not(inner))
    def _():
        pl.semaphore_wait(barrier, rows - 1 + min(cols - 1, 1))

    def hop(k, d, side):
        landing = from_left if side > 0 else from_right
        lane = 0 if side > 0 else 1
        return pltpu.make_async_remote_copy(
            src_ref=part.at[k, d],
            dst_ref=landing.at[k, d],
            send_sem=send_sem.at[k, d],
            recv_sem=recv_sem.at[lane, k, d],
            device_id={"col": me + side},
            device_id_type=MESH,
        )

    def across(k, step):
        here = out_ref.at[row, :, pl.ds(k * width, width)]
        return pltpu.make_async_remote_copy(
            src_ref=here,
            dst_ref=here,
            send_sem=row_send.at[k, step - 1],
            recv_sem=row_recv.at[k, step - 1],
            device_id={"row": lax.rem(row + step, rows)},
            device_id_type=MESH,
        )

    for k in range(CHUNKS):
        loads[k].wait()
        part[k] = lax.dot_general(
            a_ref[...], d_buf[k], (((1,), (1,)), ((), ())), preferred_element_type=jnp.float32
        ).reshape(cols, own, width)

        @pl.when(me == 0)
        def _():
            for d in range(cols - 1, 0, -1):
                hop(k, d, 1).start()

        @pl.when(me == cols - 1)
        def _():
            for d in range(cols - 1):
                hop(k, d, -1).start()

    for k in range(CHUNKS):
        for i in range(cols - 1):
            right, left = cols - 1 - i, i

            @pl.when(has_left & (me < right))
            def _():
                hop(k, right, 1).wait_recv()
                part[k, right] += from_left[k, right]
                hop(k, right, 1).start()

            @pl.when(has_right & (me > left))
            def _():
                hop(k, left, -1).wait_recv()
                part[k, left] += from_right[k, left]
                hop(k, left, -1).start()

        @pl.when(has_left)
        def _():
            hop(k, me, 1).wait_recv()
            part[k, me] += from_left[k, me]

        @pl.when(has_right)
        def _():
            hop(k, me, -1).wait_recv()
            part[k, me] += from_right[k, me]

        out_ref[row, :, k * width : (k + 1) * width] = part[k, me]
        for step in range(1, rows):
            across(k, step).start()

    for k in range(CHUNKS):
        for d in range(cols):
            @pl.when(me != d)
            def _():
                hop(k, d, 1).wait_send()
        for step in range(1, rows):
            across(k, step).wait()


def gather_hint(panel, database, cols, rows):
    row_dev, depth = database.shape
    own, width = panel.shape[0] // cols, row_dev // CHUNKS
    blocks = pltpu.VMEM((CHUNKS, cols, own, width), jnp.float32)
    return pl.pallas_call(
        functools.partial(hint_kernel, cols, rows),
        out_shape=jax.ShapeDtypeStruct((rows, own, row_dev), jnp.float32),
        in_specs=[pl.BlockSpec(memory_space=pltpu.VMEM), pl.BlockSpec(memory_space=pl.ANY)],
        out_specs=pl.BlockSpec(memory_space=pltpu.VMEM),
        scratch_shapes=[
            pltpu.VMEM((CHUNKS, width, depth), database.dtype),
            blocks,
            blocks,
            blocks,
            pltpu.SemaphoreType.DMA((CHUNKS,)),
            pltpu.SemaphoreType.DMA((CHUNKS, cols)),
            pltpu.SemaphoreType.DMA((2, CHUNKS, cols)),
            pltpu.SemaphoreType.DMA((CHUNKS, max(rows - 1, 1))),
            pltpu.SemaphoreType.DMA((CHUNKS, max(rows - 1, 1))),
        ],
        compiler_params=pltpu.CompilerParams(
            collective_id=0, has_side_effects=True, vmem_limit_bytes=48 << 20
        ),
    )(panel, database)


def sum_kernel(cols, limbs, x_ref, out_ref, landed, send_sem, recv_sem):
    col, limb = lax.axis_index("col"), lax.axis_index("limb")
    count = cols * limbs
    me = col * limbs + limb
    peers = [lax.rem(me + step, count) for step in range(1, count)]
    barrier = pltpu.get_barrier_semaphore()
    copies = []
    for step, peer in enumerate(peers):
        where = {"col": peer // limbs, "limb": lax.rem(peer, limbs)}
        pl.semaphore_signal(barrier, inc=1, device_id=where, device_id_type=MESH)
        copies.append(
            pltpu.make_async_remote_copy(
                src_ref=x_ref,
                dst_ref=landed.at[step],
                send_sem=send_sem.at[step],
                recv_sem=recv_sem.at[step],
                device_id=where,
                device_id_type=MESH,
            )
        )
    pl.semaphore_wait(barrier, count - 1)
    for copy in copies:
        copy.start()
    total = x_ref[...]
    for step, copy in enumerate(copies):
        copy.wait()
        total = total + landed[step]
    out_ref[...] = total


def sum_all(x, cols, limbs):
    peers = cols * limbs - 1
    return pl.pallas_call(
        functools.partial(sum_kernel, cols, limbs),
        out_shape=jax.ShapeDtypeStruct(x.shape, x.dtype),
        in_specs=[pl.BlockSpec(memory_space=pltpu.VMEM)],
        out_specs=pl.BlockSpec(memory_space=pltpu.VMEM),
        scratch_shapes=[
            pltpu.VMEM((peers,) + x.shape, x.dtype),
            pltpu.SemaphoreType.DMA((peers,)),
            pltpu.SemaphoreType.DMA((peers,)),
        ],
        compiler_params=pltpu.CompilerParams(collective_id=1, has_side_effects=True),
    )(x)


def tables(row_count, row_dev, fast):
    slow = row_dev // fast
    degree = row_count * row_dev
    m = np.arange(row_dev)
    t = np.arange(fast)
    angle = -2.0 * np.pi * (m[:, None] * t[None, :] % row_dev) / row_dev
    first = np.exp(1j * angle).reshape(fast, slow, fast).transpose(1, 0, 2)
    first = np.stack([first.real, first.imag], 2).astype(np.float32)
    a = np.arange(row_count)
    n = np.arange(degree)
    turn = -np.pi * (n[None, :] * (2 * a[:, None] + 1) % (2 * degree)) / degree
    turn = np.exp(1j * turn).reshape(row_count, row_count, row_dev)
    turn = np.stack([turn.real, turn.imag], 1).astype(np.float32)
    v = np.arange(slow)
    last = np.exp(-2j * np.pi * (v[:, None] * v[None, :] % slow) / slow)
    last = np.stack([last, 1j * last], 0)
    last = np.stack([last, 1j * last], 0)
    last = np.stack([last.real, last.imag], 2).astype(np.float32)
    return first, turn, last


def body(database, lwe_matrix, secret_ct):
    row_count = lax.axis_size("row")
    row_rank = lax.axis_index("row")
    col_count = lax.axis_size("col")
    row_dev = database.shape[0]
    half = lwe_matrix.shape[2]
    own = half // col_count
    fast = 128
    slow = row_dev // fast
    first, turn, last = tables(row_count, row_dev, fast)
    blocks = gather_hint(lwe_matrix[:, 0, :].T, database, col_count, row_count)
    turn = lax.dynamic_index_in_dim(jnp.asarray(turn), row_rank, 0, False)
    turned = jnp.sum(blocks[None] * turn[:, :, None, :], axis=1)
    total = jnp.einsum(
        "zjuv,vuct->vzjct",
        turned.reshape(2, own, fast, slow),
        first,
        precision=lax.Precision.HIGH,
        preferred_element_type=jnp.float32,
    )
    spec = jnp.einsum("vzjct,zcdvs->djst", total, last, precision=lax.Precision.HIGH)
    spec = spec.reshape(2, own, row_dev)
    scale = 1.0 / (math.sqrt(row_dev * row_count) * math.sqrt(2 * half))
    cipher = secret_ct[:, :, 0]
    prod_real = jnp.sum(spec[0] * cipher[:, 0] - spec[1] * cipher[:, 1], axis=1)
    prod_imag = jnp.sum(spec[0] * cipher[:, 1] + spec[1] * cipher[:, 0], axis=1)
    product = jnp.concatenate([prod_real, prod_imag], axis=0) * scale
    product = sum_all(
        product.reshape(8, -1), col_count, lax.axis_size("limb")
    ).reshape(2, 2, row_dev)
    return jnp.swapaxes(product, 0, 1)


def solution(mesh):
    placed = (P(("grp", "row"), "col"), P("col", "limb", None), P(None, None, "limb", "col", "row"))
    return jax.shard_map(
        body, mesh=mesh, in_specs=placed, out_specs=P("grp", None, "row"), check_vma=False
    )
```

profile of v0, /device:TPU:0, one launch (start us, length us, event | category | flops | bytes accessed | tf_op | source)
XLA Modules:
  0.0 118.7 jit_solution(2485836052432258754)
XLA Ops:
  0.0 0.8 dynamic-slice_bitcast_fusion
  0.8 2.9 %copy.13 = bf16[2048,1,512]{0,2,1:T(8,128)(2,1)S(1)} copy(bf16[2048,1,512]{2,0,1:T(8,128)(2,1)} %param.7) | data formatting | bytes 4194304 | tf_op args[1]
  3.7 90.2 %shard_map.64 = f32[2,128,2048]{2,1,0:T(8,128)S(1)} custom-call(bf16[512,2048]{1,0:T(8,128)(2,1)S(1)} %bitcast.50, bf16[2048,2048]{1,0:T(8,128)(2,1)} %d_hbm.1), custom_call_target="tpu_custom_call" | custom-call | tf_op jit(solution)/shard_map/pallas_call | solution.py:129
  93.9 0.4 multiply_reduce_fusion
  94.3 1.9 %copy.14 = f32[2,128,2048]{1,2,0:T(8,128)} copy(f32[2,128,2048]{2,1,0:T(8,128)S(1)} %multiply_reduce_fusion) | data formatting | bytes 4194304 | tf_op jit(solution)/shard_map/reduce_sum | solution.py:230
  96.2 0.0 copy-start.1
  96.2 4.6 %convolution_bitcast_fusion = f32[16,2,128,2,128,1]{4,2,3,1,0,5:T(8,128)S(1)} fusion(f32[16,128,2,128,1]{3,1,2,4,0:T(8,128)} %constant.25, f32[2,128,128,16,1]{1,3,2,0,4:T(8,128)} %bitcast.51), kind=kOutput, calls=%fused_computation.3 | convolution fusion | flops 805306368 | bytes 8388608 | tf_op jit(solution)/shard_map/zjuv,vuct->vzjct/dot_general | solution.py:231
  100.8 0.0 copy-done.1
  100.8 3.4 %fusion.3 = f32[2,128,16,128]{3,2,0,1:T(8,128)S(1)} fusion(f32[2,2,2,16,16,1]{3,4,0,1,2,5:T(8,128)S(1)} %copy-done.1, f32[16,2,128,2,128,1]{4,2,3,1,0,5:T(8,128)S(1)} %convolution_bitcast_fusion), kind=kOutput, calls=%fused_computation.9 | convolution fusion | flops 201326592 | bytes 6299648 | tf_op jit(solution)/shard_map/vzjct,zcdvs->djst/dot_general | solution.py:238
  104.2 0.2 fusion.6
  104.4 0.0 copy-start
  104.4 0.9 copy_bitcast_fusion
  105.3 1.3 %copy-done = f32[2,2,1,128,2048]{4,3,2,1,0:T(8,128)S(1)} copy-done((f32[2,2,1,128,2048]{4,3,2,1,0:T(8,128)S(1)}, f32[2,2,1,128,2048]{4,3,2,1,0:T(8,128)}, u32[]{:S(2)}) %copy-start) | copy-done | bytes 4194328
  106.6 0.8 subtract_reduce_fusion
  107.4 0.6 mul.71.x_ref
  108.0 9.2 %shard_map.65 = f32[8,1024]{1,0:T(8,128)} custom-call(f32[8,1024]{1,0:T(8,128)} %mul.71.x_ref), custom_call_target="tpu_custom_call" | custom-call | tf_op jit(solution)/shard_map/pallas_call | solution.py:183
  117.3 0.8 reshape.19
  118.1 0.6 copy.39
  (1 shorter events, 0.0 us)
Async XLA Ops:
  96.2 4.6 %copy-start.1 = (f32[2,2,2,16,16,1]{3,4,0,1,2,5:T(8,128)S(1)}, f32[2,2,2,16,16,1]{3,4,0,1,2,5:T(8,128)}, u32[]{:S(2)}) copy-start(f32[2,2,2,16,16,1]{3,4,0,1,2,5:T(8,128)} %constant.26) | copy-start | bytes 24580
  104.4 2.2 %copy-start = (f32[2,2,1,128,2048]{4,3,2,1,0:T(8,128)S(1)}, f32[2,2,1,128,2048]{4,3,2,1,0:T(8,128)}, u32[]{:S(2)}) copy-start(f32[2,2,1,128,2048]{4,3,2,1,0:T(8,128)} %param.8) | copy-start | bytes 12582916
where the time goes:
time: 119 us
  Pallas kernels  99.4 us (84%)
  local copies, waits for them, and re-layouts  9.95 us (8%)
  matrix products  8 us (7%)
  other arithmetic  1.23 us (1%)
    pallas_call x1, Pallas kernels, gather_hint(): pl.pallas_call(functools.partial(hint_kernel, cols, rows), out_shape=jax....  90.2 us
    pallas_call x1, Pallas kernels, sum_all(): pl.pallas_call(functools.partial(sum_kernel, cols, limbs), out_shape=jax....  9.22 us
    dot_general x1, matrix products, body(): jnp.einsum('zjuv,vuct->vzjct', turned.reshape(2, own, fast, slow), first,...  4.57 us
    unnamed x5, local copies, waits for them, and re-layouts  4.21 us
    dot_general x1, matrix products, body(): jnp.einsum('vzjct,zcdvs->djst', total, last, precision=lax.Precision.HIGH)  3.43 us

commit v1 on v0

v1 whole, which is shorter than its diff:
```python
import functools
import math

import jax
import jax.numpy as jnp
import numpy as np
from jax import lax
from jax.experimental import pallas as pl
from jax.experimental.pallas import tpu as pltpu
from jax.sharding import PartitionSpec as P

MESH = pl.DeviceIdType.MESH
UNIT = 8
LANES = 128
BLOCK = 256
EARLY = 2
LAG = 2


def fft(values):
    count = len(values)
    if count == 1:
        return values
    even, odd = fft(values[0::2]), fft(values[1::2])
    low, high = [], []
    for k in range(count // 2):
        (er, ei), (r, i) = even[k], odd[k]
        if k == 0:
            tr, ti = r, i
        elif 4 * k == count:
            tr, ti = i, -r
        elif 8 * k == count:
            half = math.sqrt(0.5)
            tr, ti = (r + i) * half, (i - r) * half
        elif 8 * k == 3 * count:
            half = math.sqrt(0.5)
            tr, ti = (i - r) * half, -(r + i) * half
        else:
            c, s = math.cos(2 * math.pi * k / count), math.sin(2 * math.pi * k / count)
            tr, ti = r * c + i * s, i * c - r * s
        low.append((er + tr, ei + ti))
        high.append((er - tr, ei - ti))
    return low + high


def swap_bits(blocks):
    blocks = list(blocks)
    lane = lax.broadcasted_iota(jnp.int32, blocks[0].shape, 1)
    step = 1
    while step < len(blocks):
        clear = (lane & step) == 0
        for b in range(len(blocks)):
            if not b & step:
                x, y = blocks[b], blocks[b + step]
                blocks[b] = jnp.where(clear, x, pltpu.roll(y, step, 1))
                blocks[b + step] = jnp.where(clear, pltpu.roll(x, LANES - step, 1), y)
        step *= 2
    return blocks


def kernel(cols, rows, grps, shared, l_hbm, d_hbm, s_hbm, turn_hbm, twiddle_hbm, w_hbm, out_ref,
           l_buf, lt, d_buf, part, from_left, from_right, land, cipher, turn, twiddle, w, acc,
           half_sum, half_in, z_in, whole_sum,
           load_sem, d_sem, send_sem, recv_sem, row_send, row_recv, s_send, s_recv, y_send, y_recv,
           limb_send, limb_recv, z_send, z_recv):
    me, row = lax.axis_index("col"), lax.axis_index("row")
    grp, limb = lax.axis_index("grp"), lax.axis_index("limb")
    units, row_dev = part.shape[1], part.shape[3]
    slow = row_dev // LANES
    blocks = d_buf.shape[0]
    first, last = me == 0, me == cols - 1
    end = first | last
    beside = jnp.where(first, 1, cols - 2)
    giver = ((me == 1) | (me == cols - 2)) if shared else None
    late = units - shared if shared else 0
    steps = max(shared + units, units + late)

    loads = [
        pltpu.make_async_copy(l_hbm, l_buf, load_sem.at[0]),
        pltpu.make_async_copy(turn_hbm.at[row], turn, load_sem.at[1]),
        pltpu.make_async_copy(twiddle_hbm, twiddle, load_sem.at[2]),
        pltpu.make_async_copy(w_hbm, w, load_sem.at[3]),
        pltpu.make_async_copy(s_hbm, cipher.at[:, :, pl.ds(0, units)], load_sem.at[4]),
    ]

    def d_load(b):
        return pltpu.make_async_copy(d_hbm.at[pl.ds(b * BLOCK, BLOCK)], d_buf.at[b], d_sem.at[b])

    loads[0].start()
    for b in range(blocks):
        d_load(b).start()
    for load in loads[1:]:
        load.start()

    barrier = pltpu.get_barrier_semaphore()
    greeted = 0
    peers = [{"col": lax.rem(me + step, cols)} for step in range(1, cols)]
    peers += [{"row": lax.rem(row + step, rows)} for step in range(1, rows)]
    peers += [{"limb": 1 - limb}]
    if shared:
        peers += [{"grp": 1 - grp}]
    for peer in peers:
        pl.semaphore_signal(barrier, inc=1, device_id=peer, device_id_type=MESH)
        greeted += 1

    acc[...] = jnp.zeros_like(acc)
    loads[0].wait()
    for c in range(0, l_buf.shape[0], BLOCK):
        lt[:, c : c + BLOCK] = l_buf[c : c + BLOCK, :].T
    pl.semaphore_wait(barrier, greeted)

    def remote(src, dst, send, recv, where):
        return pltpu.make_async_remote_copy(
            src_ref=src, dst_ref=dst, send_sem=send, recv_sem=recv, device_id=where, device_id_type=MESH
        )

    def hop(d, t, side, lanes=None):
        landing, lane = (from_left, 0) if side > 0 else (from_right, 1)
        src, dst = part.at[d, t], landing.at[d, t]
        if lanes is not None:
            src, dst = part.at[d, t, :, lanes], landing.at[d, t, :, lanes]
        return remote(src, dst, send_sem.at[lane, d, t], recv_sem.at[lane, d, t], {"col": me + side})

    def across(u, step):
        return remote(
            land.at[row, u], land.at[row, u], row_send.at[step - 1, u], row_recv.at[step - 1, u],
            {"row": lax.rem(row + step, rows)},
        )

    def give(u):
        there = jnp.where(me == 1, 0, cols - 1)
        return remote(
            s_hbm.at[grp, :, u], cipher.at[grp, :, units + u], s_send.at[u], s_recv.at[u], {"col": there}
        )

    def swap(u):
        here = cipher.at[grp, :, units + u]
        return remote(here, here, y_send.at[u], y_recv.at[u], {"grp": 1 - grp})

    if shared:
        @pl.when(giver)
        def _():
            @pl.loop(0, shared)
            def _(u):
                give(u).start()

    far = lambda side: range(cols - 1, 0, -1) if side > 0 else range(cols - 1)
    near = lambda side: (1 if side > 0 else cols - 2) if shared else None

    @pl.loop(0, blocks)
    def _(b):
        d_load(b).wait()
        lanes = pl.ds(pl.multiple_of(b * BLOCK, BLOCK), BLOCK)
        part[:, :, :, lanes] = lax.dot_general(
            lt[...], d_buf[b], (((1,), (1,)), ((), ())), preferred_element_type=jnp.float32
        ).reshape(cols, units, UNIT, BLOCK)
        for there, side in ((first, 1), (last, -1)):
            @pl.when(there)
            def _():
                for t in range(min(EARLY, units)):
                    for d in far(side):
                        if d != near(side):
                            hop(d, t, side, lanes).start()

    for there, side in ((first, 1), (last, -1)):
        @pl.when(there)
        def _():
            @pl.loop(min(EARLY, units), units)
            def _(t):
                for d in far(side):
                    if d != near(side):
                        hop(d, t, side).start()

            if shared:
                @pl.loop(shared, units)
                def _(t):
                    hop(near(side), t, side).start()

    for load in loads[1:]:
        load.wait()

    def consume(u):
        real, imag = [], []
        for s in range(slow):
            lanes = slice(s * LANES, (s + 1) * LANES)
            x = [land[m, u, :, lanes] for m in range(rows)]
            real.append(sum(x[m] * turn[m, 0, s : s + 1] for m in range(rows)))
            imag.append(sum(x[m] * turn[m, 1, s : s + 1] for m in range(rows)))
        both = jnp.concatenate([jnp.concatenate(real, 0), jnp.concatenate(imag, 0)], 1)
        high = both.astype(jnp.bfloat16)
        low = (both - high.astype(jnp.float32)).astype(jnp.bfloat16)
        mixed = jnp.dot(
            jnp.concatenate([high, low, high], 1), w[...], preferred_element_type=jnp.float32
        )
        spread = []
        for s in range(slow):
            r = mixed[s * UNIT : (s + 1) * UNIT, :LANES]
            i = mixed[s * UNIT : (s + 1) * UNIT, LANES:]
            c, n = twiddle[0, s : s + 1], twiddle[1, s : s + 1]
            spread.append((r * c - i * n, r * n + i * c) if s else (r, i))
        for v, (r, i) in enumerate(fft(spread)):
            lanes = slice(v * LANES, (v + 1) * LANES)
            for k in range(2):
                a, b = cipher[k, 0, u, :, lanes], cipher[k, 1, u, :, lanes]
                acc[k, 0, :, lanes] += r * a - i * b
                acc[k, 1, :, lanes] += r * b + i * a

    def place(i):
        at_end = jnp.where(i < shared, units + i, i - shared)
        inside = jnp.where(i < units - late, i, i - late)
        busy = jnp.where(
            end, (i >= 0) & (i < shared + units),
            (i >= 0) & ((i < units - late) | ((i >= units) & (i < units + late))),
        )
        return busy, jnp.where(end, at_end, inside)

    @pl.loop(0, steps + LAG)
    def _(i):
        @pl.when(jnp.logical_not(end) & (i < units))
        def _():
            for d in range(cols - 1, 1, -1):
                @pl.when(d > me)
                def _():
                    hop(d, i, 1).wait_recv()
                    part[d, i] += from_left[d, i]
                    hop(d, i, 1).start()
            for d in range(cols - 2):
                @pl.when(d < me)
                def _():
                    hop(d, i, -1).wait_recv()
                    part[d, i] += from_right[d, i]
                    hop(d, i, -1).start()

        busy, u = place(i)

        @pl.when(busy)
        def _():
            lent = u >= units
            d = jnp.where(lent, beside, me)
            t = jnp.where(lent, u - units, u)
            kept = t < shared

            @pl.when((me > 0) & jnp.logical_not(lent | ((me == 1) & kept)))
            def _():
                hop(me, t, 1).wait_recv()
                part[me, t] += from_left[me, t]

            @pl.when((me < cols - 1) & jnp.logical_not(lent | ((me == cols - 2) & kept)))
            def _():
                hop(me, t, -1).wait_recv()
                part[me, t] += from_right[me, t]

            moved = swap_bits(
                [part[d, t, :, b * LANES : (b + 1) * LANES] for b in range(slow)]
            )
            for s in range(slow):
                land[row, u, :, s * LANES : (s + 1) * LANES] = moved[s]
            for step in range(1, rows):
                across(u, step).start()
            if shared:
                @pl.when(lent)
                def _():
                    give(t).wait_recv()
                    swap(t).start()

        ready, v = place(i - LAG)

        @pl.when(ready)
        def _():
            for step in range(1, rows):
                across(v, step).wait_recv()
            if shared:
                @pl.when(v >= units)
                def _():
                    swap(v - units).wait_recv()
            consume(v)

    width = half_sum.shape[2]
    for k in range(2):
        for p in range(2):
            total = jnp.sum(acc[k, p], axis=0, keepdims=True)
            for q in range(4):
                r = (2 * k + p) * 2 + q % 2
                half_sum[q // 2, r : r + 1, :] = total[:, q * width : (q + 1) * width]
    other = {"limb": 1 - limb}
    trade = remote(half_sum.at[1 - limb], half_in, limb_send.at[0], limb_recv.at[0], other)
    trade.start()
    trade.wait_recv()
    z_in[me] = half_sum[limb] + half_in[...]

    def spread_to(step, peer):
        return remote(
            z_in.at[me], z_in.at[me], z_send.at[step], z_recv.at[step], {"col": peer}
        )

    for step in range(1, cols):
        spread_to(step, lax.rem(me + step, cols)).start()
    for step in range(1, cols):
        spread_to(step, lax.rem(me + step, cols)).wait_recv()
    total = z_in[0]
    for c in range(1, cols):
        total = total + z_in[c]
    whole_sum[limb] = total
    gather = remote(whole_sum.at[limb], whole_sum.at[limb], limb_send.at[1], limb_recv.at[1], other)
    gather.start()
    gather.wait_recv()
    for k in range(2):
        for p in range(2):
            for q in range(4):
                r = (2 * k + p) * 2 + q % 2
                out_ref[k, p : p + 1, q * width : (q + 1) * width] = whole_sum[q // 2, r : r + 1, :]

    for there, side in ((first, 1), (last, -1)):
        @pl.when(there)
        def _():
            @pl.loop(0, units)
            def _(t):
                for d in far(side):
                    if d != near(side):
                        hop(d, t, side).wait_send()

            if shared:
                @pl.loop(shared, units)
                def _(t):
                    hop(near(side), t, side).wait_send()

    @pl.when(jnp.logical_not(end))
    def _():
        @pl.loop(0, units)
        def _(t):
            for d in range(cols - 1, 1, -1):
                @pl.when(d > me)
                def _():
                    hop(d, t, 1).wait_send()
            for d in range(cols - 2):
                @pl.when(d < me)
                def _():
                    hop(d, t, -1).wait_send()

    if shared:
        @pl.when(giver)
        def _():
            @pl.loop(0, shared)
            def _(u):
                give(u).wait_send()

        @pl.when(end)
        def _():
            @pl.loop(0, shared)
            def _(u):
                swap(u).wait_send()
                for step in range(1, rows):
                    across(units + u, step).wait_send()

    @pl.loop(0, units)
    def _(u):
        for step in range(1, rows):
            across(u, step).wait_send()

    trade.wait_send()
    gather.wait_send()
    for step in range(1, cols):
        spread_to(step, lax.rem(me + step, cols)).wait_send()


def tables(rows, row_dev, half):
    slow = row_dev // LANES
    degree = rows * row_dev
    scale = 1.0 / (math.sqrt(degree) * math.sqrt(2 * half))
    lane = np.arange(LANES)
    at = LANES // slow * (lane % slow) + lane // slow
    n = np.arange(slow)[:, None] + slow * at[None, :]
    a, m = np.arange(rows)[:, None, None, None], np.arange(rows)[None, :, None, None]
    turn = -np.pi * ((n + m * row_dev) * (2 * a + 1) % (2 * degree)) / degree
    turn = np.exp(1j * turn) * scale
    turn = np.stack([turn.real, turn.imag], 2).astype(np.float32)
    twiddle = np.exp(-2j * np.pi * np.arange(slow)[:, None] * lane[None, :] / row_dev)
    twiddle = np.stack([twiddle.real, twiddle.imag], 0).astype(np.float32)
    w = np.exp(-2j * np.pi * (at[:, None] * lane[None, :] % LANES) / LANES)
    w = np.block([[w.real, w.imag], [-w.imag, w.real]]).astype(np.float32)
    high = w.astype(jnp.bfloat16)
    low = (w - high.astype(np.float32)).astype(jnp.bfloat16)
    return turn, twiddle, np.concatenate([high, high, low], 0)


def body(database, lwe_matrix, secret_ct):
    rows, cols = lax.axis_size("row"), lax.axis_size("col")
    grps = lax.axis_size("grp")
    row_dev, depth = database.shape
    half = lwe_matrix.shape[2]
    own = half // cols
    units = own // UNIT
    slow = row_dev // LANES
    shared = units * 5 // 8 if cols > 3 and grps == 2 else 0
    places = units + shared
    blocks = row_dev // BLOCK
    turn, twiddle, w = tables(rows, row_dev, half)
    dma = pltpu.SemaphoreType.DMA
    flow = pltpu.VMEM((cols, units, UNIT, row_dev), jnp.float32)
    lots = max(shared, 1)
    hbm = pl.BlockSpec(memory_space=pl.ANY)
    return pl.pallas_call(
        functools.partial(kernel, cols, rows, grps, shared),
        out_shape=jax.ShapeDtypeStruct((2, 2, row_dev), jnp.float32),
        in_specs=[hbm] * 6,
        out_specs=pl.BlockSpec(memory_space=pltpu.VMEM),
        scratch_shapes=[
            pltpu.VMEM((depth, half), lwe_matrix.dtype),
            pltpu.VMEM((half, depth), lwe_matrix.dtype),
            pltpu.VMEM((blocks, BLOCK, depth), database.dtype),
            flow,
            flow,
            flow,
            pltpu.VMEM((rows, places, UNIT, row_dev), jnp.float32),
            pltpu.VMEM((2, 2, places, UNIT, row_dev), jnp.float32),
            pltpu.VMEM(turn.shape[1:], jnp.float32),
            pltpu.VMEM(twiddle.shape, jnp.float32),
            pltpu.VMEM(w.shape, jnp.bfloat16),
            pltpu.VMEM((2, 2, UNIT, row_dev), jnp.float32),
            pltpu.VMEM((2, 8, row_dev // 4), jnp.float32),
            pltpu.VMEM((8, row_dev // 4), jnp.float32),
            pltpu.VMEM((cols, 8, row_dev // 4), jnp.float32),
            pltpu.VMEM((2, 8, row_dev // 4), jnp.float32),
            dma((5,)),
            dma((blocks,)),
            dma((2, cols, units)),
            dma((2, cols, units)),
            dma((max(rows - 1, 1), places)),
            dma((max(rows - 1, 1), places)),
            dma((lots,)),
            dma((lots,)),
            dma((lots,)),
            dma((lots,)),
            dma((2,)),
            dma((2,)),
            dma((cols,)),
            dma((cols,)),
        ],
        compiler_params=pltpu.CompilerParams(
            collective_id=0, has_side_effects=True, vmem_limit_bytes=56 << 20
        ),
    )(
        lwe_matrix[:, 0, :],
        database,
        secret_ct[:, :, 0].reshape(2, 2, units, UNIT, row_dev),
        jnp.asarray(turn),
        jnp.asarray(twiddle),
        jnp.asarray(w),
    )


def solution(mesh):
    placed = (P(("grp", "row"), "col"), P("col", "limb", None), P(None, None, "limb", "col", "row"))
    return jax.shard_map(
        body, mesh=mesh, in_specs=placed, out_specs=P("grp", None, "row"), check_vma=False
    )
```

time: 119 us -> 157 us (1.32)
  Pallas kernels: 99.4 us -> 155 us
  local copies, waits for them, and re-layouts: 9.95 us -> 1.38 us
  matrix products: 8 us -> 0 us
    pallas_call x2 -> x1, Pallas kernels: 99.4 us -> 155 us  [body(): pl.pallas_call(functools.partial(kernel, cols, rows, grps, shared), out_s...]
    dot_general x2 -> x0, matrix products: 8 us -> none  [the longest x1 4.57 us: body(): jnp.einsum('zjuv,vuct->vzjct', turned.reshape(2, own, fast, slow), first,...]
    unnamed x5 -> x1, local copies, waits for them, and re-layouts: 4.21 us -> 1.38 us
    mul x3 -> x0, local copies, waits for them, and re-layouts: 2.28 us -> none  [the longest x1 0.89 us: body(): prod_real = jnp.sum(spec[0] * cipher[:, 0] - spec[1] * cipher[:, 1], axis=1)]
    reduce_sum x1 -> x0, local copies, waits for them, and re-layouts: 1.87 us -> none  [body(): turned = jnp.sum(blocks[None] * turn[:, :, None, :], axis=1)]
where the time goes in v1:
time: 157 us
  Pallas kernels  155 us (99%)
    pallas_call x1, Pallas kernels, body(): pl.pallas_call(functools.partial(kernel, cols, rows, grps, shared), out_s...  155 us

profile of v1, /device:TPU:0, one launch (start us, length us, event | category | flops | bytes accessed | tf_op | source)
XLA Modules:
  0.0 156.5 jit_solution(3867065667336140235)
XLA Ops:
  0.0 155.2 %shard_map.64 = f32[2,2,2048]{2,1,0:T(2,128)} custom-call(bf16[2048,512]{1,0:T(8,128)(2,1)} %bitcast.3, bf16[2048,2048]{1,0:T(8,128)(2,1)} %d_hbm.1, f32[2,2,16,8,2048]{4,3,2,1,0:T(8,128)} %bitcast.2, f32[2,2,2,16,128]{4,3,2,1,0:T(8,128)} %constant.6.clone.turn_hbm, f32[2,16,128]{2,1,0:T(8,128)} %constant.7.clone.twiddle_hbm, ...), custom_call_target="tpu_custom_call" | custom-call | tf_op jit(solution)/shard_map/pallas_call | solution.py:402
  155.2 1.4 copy.8

commit v2 on v1

--- a/solution.py
+++ b/solution.py
@@ -14,7 +14,8 @@
 LANES = 128
 BLOCK = 256
 EARLY = 2
-LAG = 2
+LAG = 3
+HOLD = 3
 
 
 def fft(values):
@@ -73,7 +74,10 @@
     beside = jnp.where(first, 1, cols - 2)
     giver = ((me == 1) | (me == cols - 2)) if shared else None
     late = units - shared if shared else 0
-    steps = max(shared + units, units + late)
+    right_hold = HOLD * jnp.maximum(me - 1, 0)
+    left_hold = HOLD * jnp.maximum(cols - 2 - me, 0)
+    own_hold = jnp.where(end, 0, jnp.maximum(right_hold, left_hold))
+    steps = max(shared + units, units + late + HOLD * max(cols - 3, 0))
 
     loads = [
         pltpu.make_async_copy(l_hbm, l_buf, load_sem.at[0]),
@@ -216,22 +220,27 @@
 
     @pl.loop(0, steps + LAG)
     def _(i):
-        @pl.when(jnp.logical_not(end) & (i < units))
+        t_right, t_left = i - right_hold, i - left_hold
+
+        @pl.when(jnp.logical_not(end) & (t_right >= 0) & (t_right < units))
         def _():
             for d in range(cols - 1, 1, -1):
                 @pl.when(d > me)
                 def _():
-                    hop(d, i, 1).wait_recv()
-                    part[d, i] += from_left[d, i]
-                    hop(d, i, 1).start()
+                    hop(d, t_right, 1).wait_recv()
+                    part[d, t_right] += from_left[d, t_right]
+                    hop(d, t_right, 1).start()
+
+        @pl.when(jnp.logical_not(end) & (t_left >= 0) & (t_left < units))
+        def _():
             for d in range(cols - 2):
                 @pl.when(d < me)
                 def _():
-                    hop(d, i, -1).wait_recv()
-                    part[d, i] += from_right[d, i]
-                    hop(d, i, -1).start()
-
-        busy, u = place(i)
+                    hop(d, t_left, -1).wait_recv()
+                    part[d, t_left] += from_right[d, t_left]
+                    hop(d, t_left, -1).start()
+
+        busy, u = place(i - own_hold)
 
         @pl.when(busy)
         def _():
@@ -263,7 +272,7 @@
                     give(t).wait_recv()
                     swap(t).start()
 
-        ready, v = place(i - LAG)
+        ready, v = place(i - own_hold - LAG)
 
         @pl.when(ready)
         def _():

time: 157 us -> 79.7 us (0.51)
  Pallas kernels: 155 us -> 78.1 us
    pallas_call x1, Pallas kernels: 155 us -> 78.1 us  [body(): pl.pallas_call(functools.partial(kernel, cols, rows, grps, shared), out_s...]
where the time goes in v2:
time: 79.7 us; the launch traced here: 79.5 us
  Pallas kernels  78.1 us (98%)
  local copies, waits for them, and re-layouts  1.38 us (2%)
    pallas_call x1, Pallas kernels, body(): pl.pallas_call(functools.partial(kernel, cols, rows, grps, shared), out_s...  78.1 us

profile of v2, /device:TPU:0, one launch (start us, length us, event | category | flops | bytes accessed | tf_op | source)
XLA Modules:
  0.0 79.5 jit_solution(15914400780837080199)
XLA Ops:
  0.0 78.1 %shard_map.64 = f32[2,2,2048]{2,1,0:T(2,128)} custom-call(bf16[2048,512]{1,0:T(8,128)(2,1)} %bitcast.3, bf16[2048,2048]{1,0:T(8,128)(2,1)} %d_hbm.1, f32[2,2,16,8,2048]{4,3,2,1,0:T(8,128)} %bitcast.2, f32[2,2,2,16,128]{4,3,2,1,0:T(8,128)} %constant.6.clone.turn_hbm, f32[2,16,128]{2,1,0:T(8,128)} %constant.7.clone.twiddle_hbm, ...), custom_call_target="tpu_custom_call" | custom-call | tf_op jit(solution)/shard_map/pallas_call | solution.py:411
  78.2 1.4 %copy.8 = f32[2,2,2048]{2,1,0:T(2,128)} copy(f32[2,2,2048]{2,1,0:T(2,128)} %shard_map.64) | data formatting | bytes 65536

commit v3 on v2

--- a/solution.py
+++ b/solution.py
@@ -13,7 +13,9 @@
 UNIT = 8
 LANES = 128
 BLOCK = 256
-EARLY = 2
+LEAD = 4
+EARLY = 4
+PIECES = 4
 LAG = 3
 HOLD = 3
 
@@ -59,11 +61,11 @@
     return blocks
 
 
-def kernel(cols, rows, grps, shared, l_hbm, d_hbm, s_hbm, turn_hbm, twiddle_hbm, w_hbm, out_ref,
-           l_buf, lt, d_buf, part, from_left, from_right, land, cipher, turn, twiddle, w, acc,
+def kernel(cols, rows, grps, shared, l_hbm, d_hbm, s_hbm, table_hbm, w_hbm, out_ref,
+           l_buf, lt, d_buf, part, from_left, from_right, land, cipher, table, w, acc,
            half_sum, half_in, z_in, whole_sum,
            load_sem, d_sem, send_sem, recv_sem, row_send, row_recv, s_send, s_recv, y_send, y_recv,
-           limb_send, limb_recv, z_send, z_recv):
+           limb_send, limb_recv, z_send, z_recv, near_send, near_recv, bit_send, bit_recv):
     me, row = lax.axis_index("col"), lax.axis_index("row")
     grp, limb = lax.axis_index("grp"), lax.axis_index("limb")
     units, row_dev = part.shape[1], part.shape[3]
@@ -76,15 +78,18 @@
     late = units - shared if shared else 0
     right_hold = HOLD * jnp.maximum(me - 1, 0)
     left_hold = HOLD * jnp.maximum(cols - 2 - me, 0)
-    own_hold = jnp.where(end, 0, jnp.maximum(right_hold, left_hold))
-    steps = max(shared + units, units + late + HOLD * max(cols - 3, 0))
+    lag = lambda d, side: LEAD * (cols - 1 - d) if side > 0 else LEAD * d
+    by_left, by_right = right_hold + lag(me, 1), left_hold + lag(me, -1)
+    if shared:
+        by_left, by_right = jnp.where(me == 1, 0, by_left), jnp.where(me == cols - 2, 0, by_right)
+    own_hold = jnp.where(end, 0, jnp.maximum(by_left, by_right))
+    steps = max(shared + units, units + late + (HOLD + LEAD) * max(cols - 2, 0))
 
     loads = [
         pltpu.make_async_copy(l_hbm, l_buf, load_sem.at[0]),
-        pltpu.make_async_copy(turn_hbm.at[row], turn, load_sem.at[1]),
-        pltpu.make_async_copy(twiddle_hbm, twiddle, load_sem.at[2]),
-        pltpu.make_async_copy(w_hbm, w, load_sem.at[3]),
-        pltpu.make_async_copy(s_hbm, cipher.at[:, :, pl.ds(0, units)], load_sem.at[4]),
+        pltpu.make_async_copy(table_hbm.at[row], table, load_sem.at[1]),
+        pltpu.make_async_copy(w_hbm, w, load_sem.at[2]),
+        pltpu.make_async_copy(s_hbm, cipher.at[:, :, pl.ds(0, units)], load_sem.at[3]),
     ]
 
     def d_load(b):
@@ -131,6 +136,23 @@
             {"row": lax.rem(row + step, rows)},
         )
 
+    span = row_dev // PIECES
+    piece = lambda p: slice(p * span, (p + 1) * span)
+
+    def near_hop(t, p, side):
+        landing, d = (from_left, 1) if side > 0 else (from_right, cols - 2)
+        return remote(
+            part.at[d, t, :, piece(p)], landing.at[d, t, :, piece(p)],
+            near_send.at[t - shared, p], near_recv.at[t - shared, p], {"col": me + side},
+        )
+
+    def bit_across(u, step, p):
+        here = land.at[row, u, :, piece(p)]
+        return remote(
+            here, here, bit_send.at[step - 1, u - shared, p], bit_recv.at[step - 1, u - shared, p],
+            {"row": lax.rem(row + step, rows)},
+        )
+
     def give(u):
         there = jnp.where(me == 1, 0, cols - 1)
         return remote(
@@ -161,24 +183,27 @@
         for there, side in ((first, 1), (last, -1)):
             @pl.when(there)
             def _():
-                for t in range(min(EARLY, units)):
-                    for d in far(side):
-                        if d != near(side):
+                for d in far(side):
+                    if d != near(side):
+                        for t in range(min(EARLY - lag(d, side), units)):
                             hop(d, t, side, lanes).start()
 
     for there, side in ((first, 1), (last, -1)):
         @pl.when(there)
         def _():
-            @pl.loop(min(EARLY, units), units)
-            def _(t):
+            @pl.loop(EARLY, units + LEAD * (cols - 1))
+            def _(i):
                 for d in far(side):
                     if d != near(side):
-                        hop(d, t, side).start()
+                        @pl.when((i >= lag(d, side)) & (i < units + lag(d, side)))
+                        def _():
+                            hop(d, i - lag(d, side), side).start()
 
             if shared:
                 @pl.loop(shared, units)
                 def _(t):
-                    hop(near(side), t, side).start()
+                    for p in range(PIECES):
+                        near_hop(t, p, side).start()
 
     for load in loads[1:]:
         load.wait()
@@ -188,8 +213,9 @@
         for s in range(slow):
             lanes = slice(s * LANES, (s + 1) * LANES)
             x = [land[m, u, :, lanes] for m in range(rows)]
-            real.append(sum(x[m] * turn[m, 0, s : s + 1] for m in range(rows)))
-            imag.append(sum(x[m] * turn[m, 1, s : s + 1] for m in range(rows)))
+            real.append(sum(x[m] * table[2 * m + 2, s : s + 1] for m in range(rows)))
+            imag.append(sum(x[m] * table[2 * m + 3, s : s + 1] for m in range(rows)))
+        real, imag = swap_bits(real), swap_bits(imag)
         both = jnp.concatenate([jnp.concatenate(real, 0), jnp.concatenate(imag, 0)], 1)
         high = both.astype(jnp.bfloat16)
         low = (both - high.astype(jnp.float32)).astype(jnp.bfloat16)
@@ -200,7 +226,7 @@
         for s in range(slow):
             r = mixed[s * UNIT : (s + 1) * UNIT, :LANES]
             i = mixed[s * UNIT : (s + 1) * UNIT, LANES:]
-            c, n = twiddle[0, s : s + 1], twiddle[1, s : s + 1]
+            c, n = table[0, s : s + 1], table[1, s : s + 1]
             spread.append((r * c - i * n, r * n + i * c) if s else (r, i))
         for v, (r, i) in enumerate(fft(spread)):
             lanes = slice(v * LANES, (v + 1) * LANES)
@@ -218,27 +244,28 @@
         )
         return busy, jnp.where(end, at_end, inside)
 
+    def in_pieces(u):
+        return jnp.logical_not(end) & (u >= shared) & (u < units) if shared else False
+
     @pl.loop(0, steps + LAG)
     def _(i):
-        t_right, t_left = i - right_hold, i - left_hold
-
-        @pl.when(jnp.logical_not(end) & (t_right >= 0) & (t_right < units))
-        def _():
-            for d in range(cols - 1, 1, -1):
-                @pl.when(d > me)
-                def _():
-                    hop(d, t_right, 1).wait_recv()
-                    part[d, t_right] += from_left[d, t_right]
-                    hop(d, t_right, 1).start()
-
-        @pl.when(jnp.logical_not(end) & (t_left >= 0) & (t_left < units))
-        def _():
-            for d in range(cols - 2):
-                @pl.when(d < me)
-                def _():
-                    hop(d, t_left, -1).wait_recv()
-                    part[d, t_left] += from_right[d, t_left]
-                    hop(d, t_left, -1).start()
+        for d in range(cols - 1, 1, -1):
+            t = i - right_hold - lag(d, 1)
+
+            @pl.when(jnp.logical_not(end) & (d > me) & (t >= 0) & (t < units))
+            def _():
+                hop(d, t, 1).wait_recv()
+                part[d, t] += from_left[d, t]
+                hop(d, t, 1).start()
+
+        for d in range(cols - 2):
+            t = i - left_hold - lag(d, -1)
+
+            @pl.when(jnp.logical_not(end) & (d < me) & (t >= 0) & (t < units))
+            def _():
+                hop(d, t, -1).wait_recv()
+                part[d, t] += from_right[d, t]
+                hop(d, t, -1).start()
 
         busy, u = place(i - own_hold)
 
@@ -247,25 +274,39 @@
             lent = u >= units
             d = jnp.where(lent, beside, me)
             t = jnp.where(lent, u - units, u)
-            kept = t < shared
-
-            @pl.when((me > 0) & jnp.logical_not(lent | ((me == 1) & kept)))
+            whole_left, whole_right = me > 0, me < cols - 1
+            if shared:
+                whole_left, whole_right = whole_left & (me != 1), whole_right & (me != cols - 2)
+
+            @pl.when(whole_left & jnp.logical_not(lent))
             def _():
                 hop(me, t, 1).wait_recv()
                 part[me, t] += from_left[me, t]
 
-            @pl.when((me < cols - 1) & jnp.logical_not(lent | ((me == cols - 2) & kept)))
+            @pl.when(whole_right & jnp.logical_not(lent))
             def _():
                 hop(me, t, -1).wait_recv()
                 part[me, t] += from_right[me, t]
 
-            moved = swap_bits(
-                [part[d, t, :, b * LANES : (b + 1) * LANES] for b in range(slow)]
-            )
-            for s in range(slow):
-                land[row, u, :, s * LANES : (s + 1) * LANES] = moved[s]
-            for step in range(1, rows):
-                across(u, step).start()
+            @pl.when(jnp.logical_not(in_pieces(u)))
+            def _():
+                land[row, u] = part[d, t]
+                for step in range(1, rows):
+                    across(u, step).start()
+
+            if shared:
+                @pl.when(in_pieces(u))
+                def _():
+                    for p in range(PIECES):
+                        for there, side, landing in ((me == 1, 1, from_left), (me == cols - 2, -1, from_right)):
+                            @pl.when(there)
+                            def _():
+                                near_hop(u, p, side).wait_recv()
+                                part[me, u, :, piece(p)] += landing[me, u, :, piece(p)]
+                        land[row, u, :, piece(p)] = part[me, u, :, piece(p)]
+                        for step in range(1, rows):
+                            bit_across(u, step, p).start()
+
             if shared:
                 @pl.when(lent)
                 def _():
@@ -276,9 +317,18 @@
 
         @pl.when(ready)
         def _():
-            for step in range(1, rows):
-                across(v, step).wait_recv()
+            @pl.when(jnp.logical_not(in_pieces(v)))
+            def _():
+                for step in range(1, rows):
+                    across(v, step).wait_recv()
+
             if shared:
+                @pl.when(in_pieces(v))
+                def _():
+                    for step in range(1, rows):
+                        for p in range(PIECES):
+                            bit_across(v, step, p).wait_recv()
+
                 @pl.when(v >= units)
                 def _():
                     swap(v - units).wait_recv()
@@ -297,17 +347,32 @@
     trade.wait_recv()
     z_in[me] = half_sum[limb] + half_in[...]
 
-    def spread_to(step, peer):
-        return remote(
-            z_in.at[me], z_in.at[me], z_send.at[step], z_recv.at[step], {"col": peer}
-        )
-
-    for step in range(1, cols):
-        spread_to(step, lax.rem(me + step, cols)).start()
-    for step in range(1, cols):
-        spread_to(step, lax.rem(me + step, cols)).wait_recv()
-    total = z_in[0]
-    for c in range(1, cols):
+    def tell(src, dst):
+        return remote(z_in.at[src], z_in.at[src], z_send.at[dst], z_recv.at[src], {"col": dst})
+
+    tellers = range(1, cols - 1) if cols > 3 else range(cols)
+    ahead = [(me + side * step) for step in range(cols - 1, 0, -1) for side in (1, -1)]
+    if cols > 3:
+        @pl.when(end)
+        def _():
+            tell(me, beside).start()
+
+        for there, src in ((me == 1, 0), (me == cols - 2, cols - 1)):
+            @pl.when(there)
+            def _():
+                tell(src, me).wait_recv()
+                z_in[me] += z_in[src]
+
+    for dst in ahead:
+        @pl.when((jnp.logical_not(end) | (cols <= 3)) & (dst >= 0) & (dst < cols))
+        def _():
+            tell(me, dst).start()
+    for src in tellers:
+        @pl.when(me != src)
+        def _():
+            tell(src, me).wait_recv()
+    total = z_in[tellers[0]]
+    for c in tellers[1:]:
         total = total + z_in[c]
     whole_sum[limb] = total
     gather = remote(whole_sum.at[limb], whole_sum.at[limb], limb_send.at[1], limb_recv.at[1], other)
@@ -331,7 +396,8 @@
             if shared:
                 @pl.loop(shared, units)
                 def _(t):
-                    hop(near(side), t, side).wait_send()
+                    for p in range(PIECES):
+                        near_hop(t, p, side).wait_send()
 
     @pl.when(jnp.logical_not(end))
     def _():
@@ -363,13 +429,28 @@
 
     @pl.loop(0, units)
     def _(u):
-        for step in range(1, rows):
-            across(u, step).wait_send()
+        @pl.when(jnp.logical_not(in_pieces(u)))
+        def _():
+            for step in range(1, rows):
+                across(u, step).wait_send()
+
+        if shared:
+            @pl.when(in_pieces(u))
+            def _():
+                for step in range(1, rows):
+                    for p in range(PIECES):
+                        bit_across(u, step, p).wait_send()
 
     trade.wait_send()
     gather.wait_send()
-    for step in range(1, cols):
-        spread_to(step, lax.rem(me + step, cols)).wait_send()
+    if cols > 3:
+        @pl.when(end)
+        def _():
+            tell(me, beside).wait_send()
+    for dst in ahead:
+        @pl.when((jnp.logical_not(end) | (cols <= 3)) & (dst >= 0) & (dst < cols))
+        def _():
+            tell(me, dst).wait_send()
 
 
 def tables(rows, row_dev, half):
@@ -378,18 +459,20 @@
     scale = 1.0 / (math.sqrt(degree) * math.sqrt(2 * half))
     lane = np.arange(LANES)
     at = LANES // slow * (lane % slow) + lane // slow
-    n = np.arange(slow)[:, None] + slow * at[None, :]
+    n = LANES * np.arange(slow)[:, None] + lane[None, :]
     a, m = np.arange(rows)[:, None, None, None], np.arange(rows)[None, :, None, None]
     turn = -np.pi * ((n + m * row_dev) * (2 * a + 1) % (2 * degree)) / degree
     turn = np.exp(1j * turn) * scale
-    turn = np.stack([turn.real, turn.imag], 2).astype(np.float32)
+    turn = np.stack([turn.real, turn.imag], 2).reshape(rows, 2 * rows, slow, LANES)
     twiddle = np.exp(-2j * np.pi * np.arange(slow)[:, None] * lane[None, :] / row_dev)
-    twiddle = np.stack([twiddle.real, twiddle.imag], 0).astype(np.float32)
+    twiddle = np.stack([twiddle.real, twiddle.imag], 0)
+    twiddle = np.broadcast_to(twiddle, (rows,) + twiddle.shape)
+    table = np.concatenate([twiddle, turn], 1).astype(np.float32)
     w = np.exp(-2j * np.pi * (at[:, None] * lane[None, :] % LANES) / LANES)
     w = np.block([[w.real, w.imag], [-w.imag, w.real]]).astype(np.float32)
     high = w.astype(jnp.bfloat16)
     low = (w - high.astype(np.float32)).astype(jnp.bfloat16)
-    return turn, twiddle, np.concatenate([high, high, low], 0)
+    return table, np.concatenate([high, high, low], 0)
 
 
 def body(database, lwe_matrix, secret_ct):
@@ -403,7 +486,7 @@
     shared = units * 5 // 8 if cols > 3 and grps == 2 else 0
     places = units + shared
     blocks = row_dev // BLOCK
-    turn, twiddle, w = tables(rows, row_dev, half)
+    table, w = tables(rows, row_dev, half)
     dma = pltpu.SemaphoreType.DMA
     flow = pltpu.VMEM((cols, units, UNIT, row_dev), jnp.float32)
     lots = max(shared, 1)
@@ -411,7 +494,7 @@
     return pl.pallas_call(
         functools.partial(kernel, cols, rows, grps, shared),
         out_shape=jax.ShapeDtypeStruct((2, 2, row_dev), jnp.float32),
-        in_specs=[hbm] * 6,
+        in_specs=[hbm] * 5,
         out_specs=pl.BlockSpec(memory_space=pltpu.VMEM),
         scratch_shapes=[
             pltpu.VMEM((depth, half), lwe_matrix.dtype),
@@ -422,15 +505,14 @@
             flow,
             pltpu.VMEM((rows, places, UNIT, row_dev), jnp.float32),
             pltpu.VMEM((2, 2, places, UNIT, row_dev), jnp.float32),
-            pltpu.VMEM(turn.shape[1:], jnp.float32),
-            pltpu.VMEM(twiddle.shape, jnp.float32),
+            pltpu.VMEM(table.shape[1:], jnp.float32),
             pltpu.VMEM(w.shape, jnp.bfloat16),
             pltpu.VMEM((2, 2, UNIT, row_dev), jnp.float32),
             pltpu.VMEM((2, 8, row_dev // 4), jnp.float32),
             pltpu.VMEM((8, row_dev // 4), jnp.float32),
             pltpu.VMEM((cols, 8, row_dev // 4), jnp.float32),
             pltpu.VMEM((2, 8, row_dev // 4), jnp.float32),
-            dma((5,)),
+            dma((4,)),
             dma((blocks,)),
             dma((2, cols, units)),
             dma((2, cols, units)),
@@ -444,16 +526,19 @@
             dma((2,)),
             dma((cols,)),
             dma((cols,)),
+            dma((units - shared, PIECES)),
+            dma((units - shared, PIECES)),
+            dma((max(rows - 1, 1), units - shared, PIECES)),
+            dma((max(rows - 1, 1), units - shared, PIECES)),
         ],
         compiler_params=pltpu.CompilerParams(
-            collective_id=0, has_side_effects=True, vmem_limit_bytes=56 << 20
+            collective_id=0, has_side_effects=True, vmem_limit_bytes=55168 << 10
         ),
     )(
         lwe_matrix[:, 0, :],
         database,
         secret_ct[:, :, 0].reshape(2, 2, units, UNIT, row_dev),
-        jnp.asarray(turn),
-        jnp.asarray(twiddle),
+        jnp.asarray(table),
         jnp.asarray(w),
     )
 

time: 79.7 us -> 78.3 us (0.982)
  Pallas kernels: 78.1 us -> 77.2 us
    pallas_call x1, Pallas kernels: 78.1 us -> 77.2 us  [body(): pl.pallas_call(functools.partial(kernel, cols, rows, grps, shared), out_s...]
where the time goes in v3:
time: 78.3 us; the launch traced here: 77.8 us
  Pallas kernels  77.2 us (99%)
    pallas_call x1, Pallas kernels, body(): pl.pallas_call(functools.partial(kernel, cols, rows, grps, shared), out_s...  77.2 us

profile of v3, /device:TPU:0, one launch (start us, length us, event | category | flops | bytes accessed | tf_op | source)
XLA Modules:
  0.0 77.8 jit_solution(6792190823046550952)
XLA Ops:
  0.0 77.2 %shard_map.55 = f32[2,2,2048]{2,1,0:T(2,128)S(1)} custom-call(bf16[2048,512]{1,0:T(8,128)(2,1)} %bitcast.3, bf16[2048,2048]{1,0:T(8,128)(2,1)} %d_hbm.1, f32[2,2,16,8,2048]{4,3,2,1,0:T(8,128)} %bitcast.2, f32[2,6,16,128]{3,2,1,0:T(8,128)} %constant.4.clone.table_hbm, bf16[768,256]{1,0:T(8,128)(2,1)} %constant.5.clone.w_hbm), custom_call_target="tpu_custom_call" | custom-call | tf_op jit(solution)/shard_map/pallas_call | solution.py:494
  77.2 0.6 copy.7

commit v4 on v3

--- a/solution.py
+++ b/solution.py
@@ -14,8 +14,9 @@
 LANES = 128
 BLOCK = 256
 LEAD = 4
+AHEAD = 2
 EARLY = 4
-PIECES = 4
+PIECES = 2
 LAG = 3
 HOLD = 3
 
@@ -64,8 +65,8 @@
 def kernel(cols, rows, grps, shared, l_hbm, d_hbm, s_hbm, table_hbm, w_hbm, out_ref,
            l_buf, lt, d_buf, part, from_left, from_right, land, cipher, table, w, acc,
            half_sum, half_in, z_in, whole_sum,
-           load_sem, d_sem, send_sem, recv_sem, row_send, row_recv, s_send, s_recv, y_send, y_recv,
-           limb_send, limb_recv, z_send, z_recv, near_send, near_recv, bit_send, bit_recv):
+           load_sem, l_sem, d_sem, send_sem, recv_sem, row_send, row_recv, s_send, s_recv, y_send, y_recv,
+           limb_send, limb_recv, z_send, z_recv, near_send, near_recv, bit_send, bit_recv, pair_send, pair_recv):
     me, row = lax.axis_index("col"), lax.axis_index("row")
     grp, limb = lax.axis_index("grp"), lax.axis_index("limb")
     units, row_dev = part.shape[1], part.shape[3]
@@ -83,40 +84,56 @@
     if shared:
         by_left, by_right = jnp.where(me == 1, 0, by_left), jnp.where(me == cols - 2, 0, by_right)
     own_hold = jnp.where(end, 0, jnp.maximum(by_left, by_right))
-    steps = max(shared + units, units + late + (HOLD + LEAD) * max(cols - 2, 0))
+    steps = max(shared + units, units + late + 1 + (HOLD + LEAD) * max(cols - 2, 0))
+    final = units + shared
 
     loads = [
-        pltpu.make_async_copy(l_hbm, l_buf, load_sem.at[0]),
-        pltpu.make_async_copy(table_hbm.at[row], table, load_sem.at[1]),
-        pltpu.make_async_copy(w_hbm, w, load_sem.at[2]),
-        pltpu.make_async_copy(s_hbm, cipher.at[:, :, pl.ds(0, units)], load_sem.at[3]),
+        pltpu.make_async_copy(table_hbm.at[row], table, load_sem.at[0]),
+        pltpu.make_async_copy(w_hbm, w, load_sem.at[1]),
+        pltpu.make_async_copy(s_hbm, cipher.at[:, :, pl.ds(0, units)], load_sem.at[2]),
+    ]
+    chunk = l_buf.shape[0] // l_sem.shape[0]
+    l_loads = [
+        pltpu.make_async_copy(
+            l_hbm.at[pl.ds(c * chunk, chunk)], l_buf.at[pl.ds(c * chunk, chunk)], l_sem.at[c]
+        )
+        for c in range(l_sem.shape[0])
     ]
 
     def d_load(b):
         return pltpu.make_async_copy(d_hbm.at[pl.ds(b * BLOCK, BLOCK)], d_buf.at[b], d_sem.at[b])
 
-    loads[0].start()
-    for b in range(blocks):
+    for load in l_loads:
+        load.start()
+    for b in range(min(AHEAD, blocks)):
         d_load(b).start()
-    for load in loads[1:]:
-        load.start()
 
     barrier = pltpu.get_barrier_semaphore()
     greeted = 0
-    peers = [{"col": lax.rem(me + step, cols)} for step in range(1, cols)]
-    peers += [{"row": lax.rem(row + step, rows)} for step in range(1, rows)]
+    peers = [{"row": lax.rem(row + step, rows)} for step in range(1, rows)]
     peers += [{"limb": 1 - limb}]
     if shared:
         peers += [{"grp": 1 - grp}]
     for peer in peers:
         pl.semaphore_signal(barrier, inc=1, device_id=peer, device_id_type=MESH)
         greeted += 1
+    for there, side in ((me > 0, -1), (me < cols - 1, 1)):
+        @pl.when(there)
+        def _():
+            pl.semaphore_signal(barrier, inc=1, device_id={"col": me + side}, device_id_type=MESH)
 
     acc[...] = jnp.zeros_like(acc)
-    loads[0].wait()
-    for c in range(0, l_buf.shape[0], BLOCK):
-        lt[:, c : c + BLOCK] = l_buf[c : c + BLOCK, :].T
-    pl.semaphore_wait(barrier, greeted)
+    for c, load in enumerate(l_loads):
+        load.wait()
+        lt[:, c * chunk : (c + 1) * chunk] = l_buf[c * chunk : (c + 1) * chunk, :].T
+
+    @pl.when(end)
+    def _():
+        pl.semaphore_wait(barrier, greeted + min(cols - 1, 1))
+
+    @pl.when(jnp.logical_not(end))
+    def _():
+        pl.semaphore_wait(barrier, greeted + 2)
 
     def remote(src, dst, send, recv, where):
         return pltpu.make_async_remote_copy(
@@ -176,6 +193,11 @@
     @pl.loop(0, blocks)
     def _(b):
         d_load(b).wait()
+
+        @pl.when(b + AHEAD < blocks)
+        def _():
+            d_load(b + AHEAD).start()
+
         lanes = pl.ds(pl.multiple_of(b * BLOCK, BLOCK), BLOCK)
         part[:, :, :, lanes] = lax.dot_general(
             lt[...], d_buf[b], (((1,), (1,)), ((), ())), preferred_element_type=jnp.float32
@@ -200,15 +222,21 @@
                             hop(d, i - lag(d, side), side).start()
 
             if shared:
-                @pl.loop(shared, units)
+                @pl.loop(shared, units - 1)
                 def _(t):
                     for p in range(PIECES):
                         near_hop(t, p, side).start()
 
-    for load in loads[1:]:
+    for load in loads:
+        load.start()
+    for load in loads:
         load.wait()
 
-    def consume(u):
+    def pair(m):
+        here = land.at[m, final]
+        return remote(here, here, pair_send.at[m], pair_recv.at[m], {"col": beside})
+
+    def consume(u, secret):
         real, imag = [], []
         for s in range(slow):
             lanes = slice(s * LANES, (s + 1) * LANES)
@@ -231,21 +259,23 @@
         for v, (r, i) in enumerate(fft(spread)):
             lanes = slice(v * LANES, (v + 1) * LANES)
             for k in range(2):
-                a, b = cipher[k, 0, u, :, lanes], cipher[k, 1, u, :, lanes]
+                a, b = cipher[k, 0, secret, :, lanes], cipher[k, 1, secret, :, lanes]
                 acc[k, 0, :, lanes] += r * a - i * b
                 acc[k, 1, :, lanes] += r * b + i * a
 
+    extra = jnp.where(giver, 1, 0) if shared else 0
+
     def place(i):
         at_end = jnp.where(i < shared, units + i, i - shared)
-        inside = jnp.where(i < units - late, i, i - late)
+        inside = jnp.where(i < units - late, i, jnp.where(i < units + late, i - late, final))
         busy = jnp.where(
             end, (i >= 0) & (i < shared + units),
-            (i >= 0) & ((i < units - late) | ((i >= units) & (i < units + late))),
+            (i >= 0) & ((i < units - late) | ((i >= units) & (i < units + late + extra))),
         )
         return busy, jnp.where(end, at_end, inside)
 
     def in_pieces(u):
-        return jnp.logical_not(end) & (u >= shared) & (u < units) if shared else False
+        return jnp.logical_not(end) & (u >= shared) & (u < units - 1) if shared else False
 
     @pl.loop(0, steps + LAG)
     def _(i):
@@ -269,7 +299,21 @@
 
         busy, u = place(i - own_hold)
 
-        @pl.when(busy)
+        if shared:
+            @pl.when(end & (i == 0))
+            def _():
+                land[row, final] = part[beside, units - 1]
+                for step in range(1, rows):
+                    across(final, step).start()
+
+            @pl.when(end & (i == LAG))
+            def _():
+                for step in range(1, rows):
+                    across(final, step).wait_recv()
+                for m in range(rows):
+                    pair(m).start()
+
+        @pl.when(busy & (u != final))
         def _():
             lent = u >= units
             d = jnp.where(lent, beside, me)
@@ -317,7 +361,7 @@
 
         @pl.when(ready)
         def _():
-            @pl.when(jnp.logical_not(in_pieces(v)))
+            @pl.when(jnp.logical_not(in_pieces(v)) & (v != final))
             def _():
                 for step in range(1, rows):
                     across(v, step).wait_recv()
@@ -329,10 +373,15 @@
                         for p in range(PIECES):
                             bit_across(v, step, p).wait_recv()
 
-                @pl.when(v >= units)
+                @pl.when((v >= units) & (v != final))
                 def _():
                     swap(v - units).wait_recv()
-            consume(v)
+
+                @pl.when(v == final)
+                def _():
+                    for m in range(rows):
+                        pair(m).wait_recv()
+            consume(v, jnp.where(v == final, units - 1, v) if shared else v)
 
     width = half_sum.shape[2]
     for k in range(2):
@@ -394,10 +443,14 @@
                         hop(d, t, side).wait_send()
 
             if shared:
-                @pl.loop(shared, units)
+                @pl.loop(shared, units - 1)
                 def _(t):
                     for p in range(PIECES):
                         near_hop(t, p, side).wait_send()
+                for step in range(1, rows):
+                    across(final, step).wait_send()
+                for m in range(rows):
+                    pair(m).wait_send()
 
     @pl.when(jnp.logical_not(end))
     def _():
@@ -484,7 +537,7 @@
     units = own // UNIT
     slow = row_dev // LANES
     shared = units * 5 // 8 if cols > 3 and grps == 2 else 0
-    places = units + shared
+    places = units + shared + 1
     blocks = row_dev // BLOCK
     table, w = tables(rows, row_dev, half)
     dma = pltpu.SemaphoreType.DMA
@@ -504,7 +557,7 @@
             flow,
             flow,
             pltpu.VMEM((rows, places, UNIT, row_dev), jnp.float32),
-            pltpu.VMEM((2, 2, places, UNIT, row_dev), jnp.float32),
+            pltpu.VMEM((2, 2, units + shared, UNIT, row_dev), jnp.float32),
             pltpu.VMEM(table.shape[1:], jnp.float32),
             pltpu.VMEM(w.shape, jnp.bfloat16),
             pltpu.VMEM((2, 2, UNIT, row_dev), jnp.float32),
@@ -512,6 +565,7 @@
             pltpu.VMEM((8, row_dev // 4), jnp.float32),
             pltpu.VMEM((cols, 8, row_dev // 4), jnp.float32),
             pltpu.VMEM((2, 8, row_dev // 4), jnp.float32),
+            dma((3,)),
             dma((4,)),
             dma((blocks,)),
             dma((2, cols, units)),
@@ -530,6 +584,8 @@
             dma((units - shared, PIECES)),
             dma((max(rows - 1, 1), units - shared, PIECES)),
             dma((max(rows - 1, 1), units - shared, PIECES)),
+            dma((rows,)),
+            dma((rows,)),
         ],
         compiler_params=pltpu.CompilerParams(
             collective_id=0, has_side_effects=True, vmem_limit_bytes=55168 << 10

time: 78.3 us -> 79 us (level)
  no operation moved by 1% of the time
where the time goes in v4:
time: 79 us; the launch traced here: 78.5 us
  Pallas kernels  77.9 us (99%)
    pallas_call x1, Pallas kernels, body(): pl.pallas_call(functools.partial(kernel, cols, rows, grps, shared), out_s...  77.9 us

profile of v4, /device:TPU:0, one launch (start us, length us, event | category | flops | bytes accessed | tf_op | source)
XLA Modules:
  0.0 78.5 jit_solution(12010397547858546055)
XLA Ops:
  0.0 77.9 %shard_map.55 = f32[2,2,2048]{2,1,0:T(2,128)S(1)} custom-call(bf16[2048,512]{1,0:T(8,128)(2,1)} %bitcast.3, bf16[2048,2048]{1,0:T(8,128)(2,1)} %d_hbm.1, f32[2,2,16,8,2048]{4,3,2,1,0:T(8,128)} %bitcast.2, f32[2,6,16,128]{3,2,1,0:T(8,128)} %constant.4.clone.table_hbm, bf16[768,256]{1,0:T(8,128)(2,1)} %constant.5.clone.w_hbm), custom_call_target="tpu_custom_call" | custom-call | tf_op jit(solution)/shard_map/pallas_call | solution.py:547
  77.9 0.6 copy.7

commit v5 on v4

--- a/solution.py
+++ b/solution.py
@@ -18,6 +18,7 @@
 EARLY = 4
 PIECES = 2
 LAG = 3
+END_LAG = 5
 HOLD = 3
 
 
@@ -66,7 +67,7 @@
            l_buf, lt, d_buf, part, from_left, from_right, land, cipher, table, w, acc,
            half_sum, half_in, z_in, whole_sum,
            load_sem, l_sem, d_sem, send_sem, recv_sem, row_send, row_recv, s_send, s_recv, y_send, y_recv,
-           limb_send, limb_recv, z_send, z_recv, near_send, near_recv, bit_send, bit_recv, pair_send, pair_recv):
+           limb_send, limb_recv, z_send, z_recv, near_send, near_recv, bit_recv, pair_send, pair_recv):
     me, row = lax.axis_index("col"), lax.axis_index("row")
     grp, limb = lax.axis_index("grp"), lax.axis_index("limb")
     units, row_dev = part.shape[1], part.shape[3]
@@ -84,7 +85,6 @@
     if shared:
         by_left, by_right = jnp.where(me == 1, 0, by_left), jnp.where(me == cols - 2, 0, by_right)
     own_hold = jnp.where(end, 0, jnp.maximum(by_left, by_right))
-    steps = max(shared + units, units + late + 1 + (HOLD + LEAD) * max(cols - 2, 0))
     final = units + shared
 
     loads = [
@@ -107,6 +107,8 @@
         load.start()
     for b in range(min(AHEAD, blocks)):
         d_load(b).start()
+    for load in loads[:-1]:
+        load.start()
 
     barrier = pltpu.get_barrier_semaphore()
     greeted = 0
@@ -140,16 +142,24 @@
             src_ref=src, dst_ref=dst, send_sem=send, recv_sem=recv, device_id=where, device_id_type=MESH
         )
 
-    def hop(d, t, side, lanes=None):
+    def hop(d, t, side, lanes=None, to=None):
         landing, lane = (from_left, 0) if side > 0 else (from_right, 1)
         src, dst = part.at[d, t], landing.at[d, t]
         if lanes is not None:
             src, dst = part.at[d, t, :, lanes], landing.at[d, t, :, lanes]
-        return remote(src, dst, send_sem.at[lane, d, t], recv_sem.at[lane, d, t], {"col": me + side})
+        to = me + side if to is None else to
+        slot = d if side > 0 else jnp.where(d == to, cols, d)
+        return remote(src, dst, send_sem.at[lane, d], recv_sem.at[slot, t], {"col": me + side})
+
+    def arrived(d, t, side):
+        hop(d, t, side, to=me).wait_recv()
+
+    def sent(src, sem):
+        remote(src, src, sem, sem, {"col": me}).wait_send()
 
     def across(u, step):
         return remote(
-            land.at[row, u], land.at[row, u], row_send.at[step - 1, u], row_recv.at[step - 1, u],
+            land.at[row, u], land.at[row, u], row_send.at[step - 1], row_recv.at[step - 1, u],
             {"row": lax.rem(row + step, rows)},
         )
 
@@ -160,25 +170,25 @@
         landing, d = (from_left, 1) if side > 0 else (from_right, cols - 2)
         return remote(
             part.at[d, t, :, piece(p)], landing.at[d, t, :, piece(p)],
-            near_send.at[t - shared, p], near_recv.at[t - shared, p], {"col": me + side},
+            near_send.at[0], near_recv.at[t - shared, p], {"col": me + side},
         )
 
     def bit_across(u, step, p):
         here = land.at[row, u, :, piece(p)]
         return remote(
-            here, here, bit_send.at[step - 1, u - shared, p], bit_recv.at[step - 1, u - shared, p],
+            here, here, row_send.at[step - 1], bit_recv.at[step - 1, u - shared, p],
             {"row": lax.rem(row + step, rows)},
         )
 
     def give(u):
         there = jnp.where(me == 1, 0, cols - 1)
         return remote(
-            s_hbm.at[grp, :, u], cipher.at[grp, :, units + u], s_send.at[u], s_recv.at[u], {"col": there}
+            s_hbm.at[grp, :, u], cipher.at[grp, :, units + u], s_send.at[0], s_recv.at[u], {"col": there}
         )
 
     def swap(u):
         here = cipher.at[grp, :, units + u]
-        return remote(here, here, y_send.at[u], y_recv.at[u], {"grp": 1 - grp})
+        return remote(here, here, y_send.at[0], y_recv.at[u], {"grp": 1 - grp})
 
     if shared:
         @pl.when(giver)
@@ -197,6 +207,10 @@
         @pl.when(b + AHEAD < blocks)
         def _():
             d_load(b + AHEAD).start()
+
+        @pl.when(b == 1)
+        def _():
+            loads[-1].start()
 
         lanes = pl.ds(pl.multiple_of(b * BLOCK, BLOCK), BLOCK)
         part[:, :, :, lanes] = lax.dot_general(
@@ -228,13 +242,11 @@
                         near_hop(t, p, side).start()
 
     for load in loads:
-        load.start()
-    for load in loads:
         load.wait()
 
     def pair(m):
         here = land.at[m, final]
-        return remote(here, here, pair_send.at[m], pair_recv.at[m], {"col": beside})
+        return remote(here, here, pair_send.at[0], pair_recv.at[m], {"col": beside})
 
     def consume(u, secret):
         real, imag = [], []
@@ -267,7 +279,8 @@
 
     def place(i):
         at_end = jnp.where(i < shared, units + i, i - shared)
-        inside = jnp.where(i < units - late, i, jnp.where(i < units + late, i - late, final))
+        after = jnp.where(i == units, units - 1, jnp.where(i < units + late, i - late - 1, final))
+        inside = jnp.where(i < units - late, i, after)
         busy = jnp.where(
             end, (i >= 0) & (i < shared + units),
             (i >= 0) & ((i < units - late) | ((i >= units) & (i < units + late + extra))),
@@ -277,26 +290,30 @@
     def in_pieces(u):
         return jnp.logical_not(end) & (u >= shared) & (u < units - 1) if shared else False
 
-    @pl.loop(0, steps + LAG)
-    def _(i):
+    wait = jnp.where(end, END_LAG, LAG)
+    rest = jnp.maximum(
+        right_hold + LEAD * jnp.maximum(cols - 2 - me, 0), left_hold + LEAD * jnp.maximum(me - 1, 0)
+    )
+    rest = jnp.maximum(rest, own_hold + late + extra + LAG)
+    steps = units + jnp.where(end, shared + END_LAG, rest)
+
+    def forward(d, side, i):
+        beyond, hold, landing = (
+            (d > me, right_hold, from_left) if side > 0 else (d < me, left_hold, from_right)
+        )
+        t = i - hold - lag(d, side)
+
+        @pl.when(jnp.logical_not(end) & beyond & (t >= 0) & (t < units))
+        def _():
+            arrived(d, t, side)
+            part[d, t] += landing[d, t]
+            hop(d, t, side).start()
+
+    def step_of(i, carry):
         for d in range(cols - 1, 1, -1):
-            t = i - right_hold - lag(d, 1)
-
-            @pl.when(jnp.logical_not(end) & (d > me) & (t >= 0) & (t < units))
-            def _():
-                hop(d, t, 1).wait_recv()
-                part[d, t] += from_left[d, t]
-                hop(d, t, 1).start()
-
+            forward(d, 1, i)
         for d in range(cols - 2):
-            t = i - left_hold - lag(d, -1)
-
-            @pl.when(jnp.logical_not(end) & (d < me) & (t >= 0) & (t < units))
-            def _():
-                hop(d, t, -1).wait_recv()
-                part[d, t] += from_right[d, t]
-                hop(d, t, -1).start()
-
+            forward(d, -1, i)
         busy, u = place(i - own_hold)
 
         if shared:
@@ -324,12 +341,12 @@
 
             @pl.when(whole_left & jnp.logical_not(lent))
             def _():
-                hop(me, t, 1).wait_recv()
+                arrived(me, t, 1)
                 part[me, t] += from_left[me, t]
 
             @pl.when(whole_right & jnp.logical_not(lent))
             def _():
-                hop(me, t, -1).wait_recv()
+                arrived(me, t, -1)
                 part[me, t] += from_right[me, t]
 
             @pl.when(jnp.logical_not(in_pieces(u)))
@@ -357,7 +374,7 @@
                     give(t).wait_recv()
                     swap(t).start()
 
-        ready, v = place(i - own_hold - LAG)
+        ready, v = place(i - own_hold - wait)
 
         @pl.when(ready)
         def _():
@@ -382,6 +399,10 @@
                     for m in range(rows):
                         pair(m).wait_recv()
             consume(v, jnp.where(v == final, units - 1, v) if shared else v)
+
+        return carry
+
+    lax.fori_loop(0, steps, step_of, 0)
 
     width = half_sum.shape[2]
     for k in range(2):
@@ -397,7 +418,7 @@
     z_in[me] = half_sum[limb] + half_in[...]
 
     def tell(src, dst):
-        return remote(z_in.at[src], z_in.at[src], z_send.at[dst], z_recv.at[src], {"col": dst})
+        return remote(z_in.at[src], z_in.at[src], z_send.at[0], z_recv.at[src], {"col": dst})
 
     tellers = range(1, cols - 1) if cols > 3 else range(cols)
     ahead = [(me + side * step) for step in range(cols - 1, 0, -1) for side in (1, -1)]
@@ -416,6 +437,39 @@
         @pl.when((jnp.logical_not(end) | (cols <= 3)) & (dst >= 0) & (dst < cols))
         def _():
             tell(me, dst).start()
+    for there, side in ((first, 1), (last, -1)):
+        @pl.when(there)
+        def _():
+            lane = 0 if side > 0 else 1
+            for d in far(side):
+                if d != near(side):
+                    sent(part.at[d], send_sem.at[lane, d])
+            for step in range(1, rows):
+                sent(land.at[row, pl.ds(0, final + 1 if shared else units)], row_send.at[step - 1])
+            if shared:
+                if units - 1 > shared:
+                    sent(part.at[near(side), pl.ds(shared, units - 1 - shared)], near_send.at[0])
+                sent(land.at[:, final], pair_send.at[0])
+                sent(cipher.at[grp, :, pl.ds(units, shared)], y_send.at[0])
+
+    @pl.when(jnp.logical_not(end))
+    def _():
+        for d in range(cols - 1, 1, -1):
+            @pl.when(d > me)
+            def _():
+                sent(part.at[d], send_sem.at[0, d])
+        for d in range(cols - 2):
+            @pl.when(d < me)
+            def _():
+                sent(part.at[d], send_sem.at[1, d])
+        for step in range(1, rows):
+            sent(land.at[row, pl.ds(0, units)], row_send.at[step - 1])
+
+    if shared:
+        @pl.when(giver)
+        def _():
+            sent(cipher.at[grp, :, pl.ds(units, shared)], s_send.at[0])
+
     for src in tellers:
         @pl.when(me != src)
         def _():
@@ -433,77 +487,18 @@
                 r = (2 * k + p) * 2 + q % 2
                 out_ref[k, p : p + 1, q * width : (q + 1) * width] = whole_sum[q // 2, r : r + 1, :]
 
-    for there, side in ((first, 1), (last, -1)):
-        @pl.when(there)
-        def _():
-            @pl.loop(0, units)
-            def _(t):
-                for d in far(side):
-                    if d != near(side):
-                        hop(d, t, side).wait_send()
-
-            if shared:
-                @pl.loop(shared, units - 1)
-                def _(t):
-                    for p in range(PIECES):
-                        near_hop(t, p, side).wait_send()
-                for step in range(1, rows):
-                    across(final, step).wait_send()
-                for m in range(rows):
-                    pair(m).wait_send()
-
-    @pl.when(jnp.logical_not(end))
-    def _():
-        @pl.loop(0, units)
-        def _(t):
-            for d in range(cols - 1, 1, -1):
-                @pl.when(d > me)
-                def _():
-                    hop(d, t, 1).wait_send()
-            for d in range(cols - 2):
-                @pl.when(d < me)
-                def _():
-                    hop(d, t, -1).wait_send()
-
-    if shared:
-        @pl.when(giver)
-        def _():
-            @pl.loop(0, shared)
-            def _(u):
-                give(u).wait_send()
-
-        @pl.when(end)
-        def _():
-            @pl.loop(0, shared)
-            def _(u):
-                swap(u).wait_send()
-                for step in range(1, rows):
-                    across(units + u, step).wait_send()
-
-    @pl.loop(0, units)
-    def _(u):
-        @pl.when(jnp.logical_not(in_pieces(u)))
-        def _():
-            for step in range(1, rows):
-                across(u, step).wait_send()
-
-        if shared:
-            @pl.when(in_pieces(u))
-            def _():
-                for step in range(1, rows):
-                    for p in range(PIECES):
-                        bit_across(u, step, p).wait_send()
-
     trade.wait_send()
     gather.wait_send()
     if cols > 3:
         @pl.when(end)
         def _():
-            tell(me, beside).wait_send()
-    for dst in ahead:
-        @pl.when((jnp.logical_not(end) | (cols <= 3)) & (dst >= 0) & (dst < cols))
-        def _():
-            tell(me, dst).wait_send()
+            sent(z_in.at[0], z_send.at[0])
+
+        @pl.when(jnp.logical_not(end))
+        def _():
+            sent(z_in.at[pl.ds(0, cols - 1)], z_send.at[0])
+    elif cols > 1:
+        sent(z_in.at[pl.ds(0, cols - 1)], z_send.at[0])
 
 
 def tables(rows, row_dev, half):
@@ -536,7 +531,7 @@
     own = half // cols
     units = own // UNIT
     slow = row_dev // LANES
-    shared = units * 5 // 8 if cols > 3 and grps == 2 else 0
+    shared = units * 11 // 16 if cols > 3 and grps == 2 else 0
     places = units + shared + 1
     blocks = row_dev // BLOCK
     table, w = tables(rows, row_dev, half)
@@ -568,23 +563,22 @@
             dma((3,)),
             dma((4,)),
             dma((blocks,)),
-            dma((2, cols, units)),
-            dma((2, cols, units)),
+            dma((2, cols)),
+            dma((cols + 1, units)),
+            dma((max(rows - 1, 1),)),
             dma((max(rows - 1, 1), places)),
-            dma((max(rows - 1, 1), places)),
+            dma((1,)),
             dma((lots,)),
-            dma((lots,)),
-            dma((lots,)),
+            dma((1,)),
             dma((lots,)),
             dma((2,)),
             dma((2,)),
+            dma((1,)),
             dma((cols,)),
-            dma((cols,)),
-            dma((units - shared, PIECES)),
-            dma((units - shared, PIECES)),
-            dma((max(rows - 1, 1), units - shared, PIECES)),
-            dma((max(rows - 1, 1), units - shared, PIECES)),
-            dma((rows,)),
+            dma((1,)),
+            dma((max(units - 1 - shared, 1), PIECES)),
+            dma((max(rows - 1, 1), max(units - 1 - shared, 1), PIECES)),
+            dma((1,)),
             dma((rows,)),
         ],
         compiler_params=pltpu.CompilerParams(

time: 79 us -> 76.2 us (0.965)
  Pallas kernels: 77.9 us -> 75.5 us
    pallas_call x1, Pallas kernels: 77.9 us -> 75.5 us  [body(): pl.pallas_call(functools.partial(kernel, cols, rows, grps, shared), out_s...]
where the time goes in v5:
time: 76.2 us; the launch traced here: 76.1 us
  Pallas kernels  75.5 us (99%)
    pallas_call x1, Pallas kernels, body(): pl.pallas_call(functools.partial(kernel, cols, rows, grps, shared), out_s...  75.5 us

profile of v5, /device:TPU:0, one launch (start us, length us, event | category | flops | bytes accessed | tf_op | source)
XLA Modules:
  0.0 76.1 jit_solution(10429328980686273425)
XLA Ops:
  0.0 75.5 %shard_map.55 = f32[2,2,2048]{2,1,0:T(2,128)S(1)} custom-call(bf16[2048,512]{1,0:T(8,128)(2,1)} %bitcast.3, bf16[2048,2048]{1,0:T(8,128)(2,1)} %d_hbm.1, f32[2,2,16,8,2048]{4,3,2,1,0:T(8,128)} %bitcast.2, f32[2,6,16,128]{3,2,1,0:T(8,128)} %constant.4.clone.table_hbm, bf16[768,256]{1,0:T(8,128)(2,1)} %constant.5.clone.w_hbm), custom_call_target="tpu_custom_call" | custom-call | tf_op jit(solution)/shard_map/pallas_call | solution.py:542
  75.5 0.6 copy.7

commit v6 on v5

--- a/solution.py
+++ b/solution.py
@@ -16,6 +16,7 @@
 LEAD = 4
 AHEAD = 2
 EARLY = 4
+DELAY = 3
 PIECES = 2
 LAG = 3
 END_LAG = 5
@@ -67,7 +68,7 @@
            l_buf, lt, d_buf, part, from_left, from_right, land, cipher, table, w, acc,
            half_sum, half_in, z_in, whole_sum,
            load_sem, l_sem, d_sem, send_sem, recv_sem, row_send, row_recv, s_send, s_recv, y_send, y_recv,
-           limb_send, limb_recv, z_send, z_recv, near_send, near_recv, bit_recv, pair_send, pair_recv):
+           limb_send, limb_recv, z_send, z_recv, near_send, near_recv, bit_recv, pair_send, pair_recv, early_recv):
     me, row = lax.axis_index("col"), lax.axis_index("row")
     grp, limb = lax.axis_index("grp"), lax.axis_index("limb")
     units, row_dev = part.shape[1], part.shape[3]
@@ -142,11 +143,21 @@
             src_ref=src, dst_ref=dst, send_sem=send, recv_sem=recv, device_id=where, device_id_type=MESH
         )
 
-    def hop(d, t, side, lanes=None, to=None):
+    early = min(EARLY, units)
+    farthest = lambda side: cols - 1 if side > 0 else 0
+
+    def early_hop(b, side):
+        landing, lane = (from_left, 0) if side > 0 else (from_right, 1)
+        lanes = pl.ds(pl.multiple_of(b * BLOCK, BLOCK), BLOCK)
+        d = farthest(side)
+        return remote(
+            part.at[d, pl.ds(0, early), :, lanes], landing.at[d, pl.ds(0, early), :, lanes],
+            send_sem.at[lane, d], early_recv.at[lane, b], {"col": me + side},
+        )
+
+    def hop(d, t, side, to=None):
         landing, lane = (from_left, 0) if side > 0 else (from_right, 1)
         src, dst = part.at[d, t], landing.at[d, t]
-        if lanes is not None:
-            src, dst = part.at[d, t, :, lanes], landing.at[d, t, :, lanes]
         to = me + side if to is None else to
         slot = d if side > 0 else jnp.where(d == to, cols, d)
         return remote(src, dst, send_sem.at[lane, d], recv_sem.at[slot, t], {"col": me + side})
@@ -200,34 +211,48 @@
     far = lambda side: range(cols - 1, 0, -1) if side > 0 else range(cols - 1)
     near = lambda side: (1 if side > 0 else cols - 2) if shared else None
 
-    @pl.loop(0, blocks)
-    def _(b):
-        d_load(b).wait()
-
-        @pl.when(b + AHEAD < blocks)
-        def _():
-            d_load(b + AHEAD).start()
-
-        @pl.when(b == 1)
-        def _():
-            loads[-1].start()
-
-        lanes = pl.ds(pl.multiple_of(b * BLOCK, BLOCK), BLOCK)
-        part[:, :, :, lanes] = lax.dot_general(
-            lt[...], d_buf[b], (((1,), (1,)), ((), ())), preferred_element_type=jnp.float32
-        ).reshape(cols, units, UNIT, BLOCK)
-        for there, side in ((first, 1), (last, -1)):
-            @pl.when(there)
-            def _():
-                for d in far(side):
-                    if d != near(side):
-                        for t in range(min(EARLY - lag(d, side), units)):
-                            hop(d, t, side, lanes).start()
+    def block(b, carry):
+        @pl.when(b < blocks)
+        def _():
+            d_load(b).wait()
+
+            @pl.when(b + AHEAD < blocks)
+            def _():
+                d_load(b + AHEAD).start()
+
+            @pl.when(b == 1)
+            def _():
+                loads[-1].start()
+
+            lanes = pl.ds(pl.multiple_of(b * BLOCK, BLOCK), BLOCK)
+            part[:, :, :, lanes] = lax.dot_general(
+                lt[...], d_buf[b], (((1,), (1,)), ((), ())), preferred_element_type=jnp.float32
+            ).reshape(cols, units, UNIT, BLOCK)
+            if cols > 1:
+                for there, side in ((first, 1), (last, -1)):
+                    @pl.when(there)
+                    def _():
+                        early_hop(b, side).start()
+
+        for side, hops, landing in ((1, me, from_left), (-1, cols - 1 - me, from_right)):
+            c = b - DELAY * hops
+
+            @pl.when(jnp.logical_not(end) & (c >= 0) & (c < blocks))
+            def _():
+                early_hop(c, side).wait_recv()
+                d, lanes = farthest(side), pl.ds(pl.multiple_of(c * BLOCK, BLOCK), BLOCK)
+                part[d, 0:early, :, lanes] += landing[d, 0:early, :, lanes]
+                early_hop(c, side).start()
+
+        return carry
+
+    follow = jnp.where(end, 0, DELAY * jnp.maximum(me, cols - 1 - me))
+    lax.fori_loop(0, blocks + follow, block, 0)
 
     for there, side in ((first, 1), (last, -1)):
         @pl.when(there)
         def _():
-            @pl.loop(EARLY, units + LEAD * (cols - 1))
+            @pl.loop(early, units + LEAD * (cols - 1))
             def _(i):
                 for d in far(side):
                     if d != near(side):
@@ -276,14 +301,19 @@
                 acc[k, 1, :, lanes] += r * b + i * a
 
     extra = jnp.where(giver, 1, 0) if shared else 0
+    late_from = jnp.maximum(units + LEAD, shared + own_hold)
 
     def place(i):
         at_end = jnp.where(i < shared, units + i, i - shared)
-        after = jnp.where(i == units, units - 1, jnp.where(i < units + late, i - late - 1, final))
-        inside = jnp.where(i < units - late, i, after)
+        m = i - late_from
+        inside = jnp.where(m < 0, i - own_hold, shared + m)
+        if late > 1:
+            inside = jnp.where(m == late - 2, units - 1, jnp.where(m == late - 1, units - 2, inside))
+        if late:
+            inside = jnp.where(m == late, final, inside)
+        early_ones = (i >= own_hold) & (i < own_hold + units - late)
         busy = jnp.where(
-            end, (i >= 0) & (i < shared + units),
-            (i >= 0) & ((i < units - late) | ((i >= units) & (i < units + late + extra))),
+            end, (i >= 0) & (i < shared + units), early_ones | ((m >= 0) & (m < late + extra))
         )
         return busy, jnp.where(end, at_end, inside)
 
@@ -294,8 +324,10 @@
     rest = jnp.maximum(
         right_hold + LEAD * jnp.maximum(cols - 2 - me, 0), left_hold + LEAD * jnp.maximum(me - 1, 0)
     )
-    rest = jnp.maximum(rest, own_hold + late + extra + LAG)
-    steps = units + jnp.where(end, shared + END_LAG, rest)
+    rest = jnp.maximum(units + rest, own_hold + units - late + LAG)
+    if late:
+        rest = jnp.maximum(rest, late_from + late + extra + LAG)
+    steps = jnp.where(end, shared + units + END_LAG, rest)
 
     def forward(d, side, i):
         beyond, hold, landing = (
@@ -303,7 +335,7 @@
         )
         t = i - hold - lag(d, side)
 
-        @pl.when(jnp.logical_not(end) & beyond & (t >= 0) & (t < units))
+        @pl.when(jnp.logical_not(end) & beyond & (t >= (early if d == farthest(side) else 0)) & (t < units))
         def _():
             arrived(d, t, side)
             part[d, t] += landing[d, t]
@@ -314,7 +346,7 @@
             forward(d, 1, i)
         for d in range(cols - 2):
             forward(d, -1, i)
-        busy, u = place(i - own_hold)
+        busy, u = place(i)
 
         if shared:
             @pl.when(end & (i == 0))
@@ -339,14 +371,31 @@
             if shared:
                 whole_left, whole_right = whole_left & (me != 1), whole_right & (me != cols - 2)
 
+            @pl.when(end & (u == 0) & (cols > 1))
+            def _():
+                for there, side in ((last, 1), (first, -1)):
+                    @pl.when(there)
+                    def _():
+                        @pl.loop(0, blocks)
+                        def _(b):
+                            early_hop(b, side).wait_recv()
+
+            by_blocks = end & (t < early)
+
             @pl.when(whole_left & jnp.logical_not(lent))
             def _():
-                arrived(me, t, 1)
+                @pl.when(jnp.logical_not(by_blocks))
+                def _():
+                    arrived(me, t, 1)
+
                 part[me, t] += from_left[me, t]
 
             @pl.when(whole_right & jnp.logical_not(lent))
             def _():
-                arrived(me, t, -1)
+                @pl.when(jnp.logical_not(by_blocks))
+                def _():
+                    arrived(me, t, -1)
+
                 part[me, t] += from_right[me, t]
 
             @pl.when(jnp.logical_not(in_pieces(u)))
@@ -374,7 +423,7 @@
                     give(t).wait_recv()
                     swap(t).start()
 
-        ready, v = place(i - own_hold - wait)
+        ready, v = place(i - wait)
 
         @pl.when(ready)
         def _():
@@ -531,7 +580,7 @@
     own = half // cols
     units = own // UNIT
     slow = row_dev // LANES
-    shared = units * 11 // 16 if cols > 3 and grps == 2 else 0
+    shared = units * 10 // 16 if cols > 3 and grps == 2 else 0
     places = units + shared + 1
     blocks = row_dev // BLOCK
     table, w = tables(rows, row_dev, half)
@@ -580,6 +629,7 @@
             dma((max(rows - 1, 1), max(units - 1 - shared, 1), PIECES)),
             dma((1,)),
             dma((rows,)),
+            dma((2, blocks)),
         ],
         compiler_params=pltpu.CompilerParams(
             collective_id=0, has_side_effects=True, vmem_limit_bytes=55168 << 10

time: 76.2 us -> 74.5 us (0.978)
  Pallas kernels: 75.5 us -> 73.7 us
    pallas_call x1, Pallas kernels: 75.5 us -> 73.7 us  [body(): pl.pallas_call(functools.partial(kernel, cols, rows, grps, shared), out_s...]
where the time goes in v6:
time: 74.5 us; the launch traced here: 74.3 us
  Pallas kernels  73.7 us (99%)
    pallas_call x1, Pallas kernels, body(): pl.pallas_call(functools.partial(kernel, cols, rows, grps, shared), out_s...  73.7 us

profile of v6, /device:TPU:0, one launch (start us, length us, event | category | flops | bytes accessed | tf_op | source)
XLA Modules:
  0.0 74.3 jit_solution(12543718587441142503)
XLA Ops:
  0.0 73.7 %shard_map.55 = f32[2,2,2048]{2,1,0:T(2,128)S(1)} custom-call(bf16[2048,512]{1,0:T(8,128)(2,1)} %bitcast.3, bf16[2048,2048]{1,0:T(8,128)(2,1)} %d_hbm.1, f32[2,2,16,8,2048]{4,3,2,1,0:T(8,128)} %bitcast.2, f32[2,6,16,128]{3,2,1,0:T(8,128)} %constant.4.clone.table_hbm, bf16[768,256]{1,0:T(8,128)(2,1)} %constant.5.clone.w_hbm), custom_call_target="tpu_custom_call" | custom-call | tf_op jit(solution)/shard_map/pallas_call | solution.py:591
  73.7 0.6 copy.7

commit v7 on v6

--- a/solution.py
+++ b/solution.py
@@ -14,10 +14,11 @@
 LANES = 128
 BLOCK = 256
 LEAD = 4
-AHEAD = 2
+AHEAD = 4
 EARLY = 4
-DELAY = 3
-PIECES = 2
+NEXT = 2
+DELAY = 4
+PIECES = 1
 LAG = 3
 END_LAG = 5
 HOLD = 3
@@ -65,7 +66,7 @@
 
 
 def kernel(cols, rows, grps, shared, l_hbm, d_hbm, s_hbm, table_hbm, w_hbm, out_ref,
-           l_buf, lt, d_buf, part, from_left, from_right, land, cipher, table, w, acc,
+           l_buf, lt_outer, lt_inner, d_buf, part, from_left, from_right, land, cipher, table, w, acc,
            half_sum, half_in, z_in, whole_sum,
            load_sem, l_sem, d_sem, send_sem, recv_sem, row_send, row_recv, s_send, s_recv, y_send, y_recv,
            limb_send, limb_recv, z_send, z_recv, near_send, near_recv, bit_recv, pair_send, pair_recv, early_recv):
@@ -93,21 +94,31 @@
         pltpu.make_async_copy(w_hbm, w, load_sem.at[1]),
         pltpu.make_async_copy(s_hbm, cipher.at[:, :, pl.ds(0, units)], load_sem.at[2]),
     ]
-    chunk = l_buf.shape[0] // l_sem.shape[0]
-    l_loads = [
-        pltpu.make_async_copy(
-            l_hbm.at[pl.ds(c * chunk, chunk)], l_buf.at[pl.ds(c * chunk, chunk)], l_sem.at[c]
-        )
-        for c in range(l_sem.shape[0])
-    ]
+    chunks = l_sem.shape[0]
+    chunk = l_buf.shape[1] // chunks
+    outer = [0, chunks - 1] if chunks > 1 else [0]
+    inner = list(range(1, chunks - 1))
+    held = chunk * cols // l_buf.shape[1]
+
+    def l_load(c):
+        there = pl.ds(c * chunk, chunk)
+        return pltpu.make_async_copy(l_hbm.at[:, there], l_buf.at[:, there], l_sem.at[c])
+
+    def turn_over(c, lt, at):
+        l_load(c).wait()
+        lt[at * chunk : (at + 1) * chunk, :] = l_buf[:, c * chunk : (c + 1) * chunk].T
 
     def d_load(b):
-        return pltpu.make_async_copy(d_hbm.at[pl.ds(b * BLOCK, BLOCK)], d_buf.at[b], d_sem.at[b])
-
-    for load in l_loads:
-        load.start()
+        return pltpu.make_async_copy(
+            d_hbm.at[pl.ds(b * BLOCK, BLOCK)], d_buf.at[b], d_sem.at[lax.rem(b, AHEAD)]
+        )
+
+    for c in outer:
+        l_load(c).start()
     for b in range(min(AHEAD, blocks)):
         d_load(b).start()
+    for c in inner:
+        l_load(c).start()
     for load in loads[:-1]:
         load.start()
 
@@ -126,9 +137,8 @@
             pl.semaphore_signal(barrier, inc=1, device_id={"col": me + side}, device_id_type=MESH)
 
     acc[...] = jnp.zeros_like(acc)
-    for c, load in enumerate(l_loads):
-        load.wait()
-        lt[:, c * chunk : (c + 1) * chunk] = l_buf[c * chunk : (c + 1) * chunk, :].T
+    for at, c in enumerate(outer):
+        turn_over(c, lt_outer, at)
 
     @pl.when(end)
     def _():
@@ -143,7 +153,7 @@
             src_ref=src, dst_ref=dst, send_sem=send, recv_sem=recv, device_id=where, device_id_type=MESH
         )
 
-    early = min(EARLY, units)
+    early, ahead_of_rest = min(EARLY, units), min(EARLY + NEXT, units)
     farthest = lambda side: cols - 1 if side > 0 else 0
 
     def early_hop(b, side):
@@ -159,7 +169,7 @@
         landing, lane = (from_left, 0) if side > 0 else (from_right, 1)
         src, dst = part.at[d, t], landing.at[d, t]
         to = me + side if to is None else to
-        slot = d if side > 0 else jnp.where(d == to, cols, d)
+        slot = d if side > 0 or recv_sem.shape[0] == cols else jnp.where(d == to, cols, d)
         return remote(src, dst, send_sem.at[lane, d], recv_sem.at[slot, t], {"col": me + side})
 
     def arrived(d, t, side):
@@ -211,6 +221,12 @@
     far = lambda side: range(cols - 1, 0, -1) if side > 0 else range(cols - 1)
     near = lambda side: (1 if side > 0 else cols - 2) if shared else None
 
+    def product(lt, b):
+        found = lax.dot_general(
+            lt[...], d_buf[b], (((1,), (1,)), ((), ())), preferred_element_type=jnp.float32
+        )
+        return found.reshape(-1, units, UNIT, BLOCK)
+
     def block(b, carry):
         @pl.when(b < blocks)
         def _():
@@ -220,20 +236,35 @@
             def _():
                 d_load(b + AHEAD).start()
 
-            @pl.when(b == 1)
-            def _():
-                loads[-1].start()
-
             lanes = pl.ds(pl.multiple_of(b * BLOCK, BLOCK), BLOCK)
-            part[:, :, :, lanes] = lax.dot_general(
-                lt[...], d_buf[b], (((1,), (1,)), ((), ())), preferred_element_type=jnp.float32
-            ).reshape(cols, units, UNIT, BLOCK)
+            found = product(lt_outer, b)
+            for at, c in enumerate(outer):
+                part[c * held : (c + 1) * held, :, :, lanes] = found[at * held : (at + 1) * held]
             if cols > 1:
                 for there, side in ((first, 1), (last, -1)):
                     @pl.when(there)
                     def _():
                         early_hop(b, side).start()
 
+        @pl.when(b == blocks)
+        def _():
+            if cols > 1:
+                for there, side in ((first, 1), (last, -1)):
+                    @pl.when(there)
+                    def _():
+                        for t in range(early, ahead_of_rest):
+                            hop(farthest(side), t, side).start()
+
+            loads[-1].start()
+            for at, c in enumerate(inner):
+                turn_over(c, lt_inner, at)
+
+        if inner:
+            @pl.when((b >= blocks) & (b < 2 * blocks))
+            def _():
+                lanes = pl.ds(pl.multiple_of((b - blocks) * BLOCK, BLOCK), BLOCK)
+                part[held : cols - held, :, :, lanes] = product(lt_inner, b - blocks)
+
         for side, hops, landing in ((1, me, from_left), (-1, cols - 1 - me, from_right)):
             c = b - DELAY * hops
 
@@ -247,18 +278,20 @@
         return carry
 
     follow = jnp.where(end, 0, DELAY * jnp.maximum(me, cols - 1 - me))
-    lax.fori_loop(0, blocks + follow, block, 0)
+    lax.fori_loop(0, blocks + jnp.maximum(follow, blocks), block, 0)
 
     for there, side in ((first, 1), (last, -1)):
         @pl.when(there)
         def _():
-            @pl.loop(early, units + LEAD * (cols - 1))
+            @pl.loop(min(early, LEAD), units + LEAD * (cols - 1))
             def _(i):
                 for d in far(side):
                     if d != near(side):
-                        @pl.when((i >= lag(d, side)) & (i < units + lag(d, side)))
+                        t = i - lag(d, side)
+
+                        @pl.when((t >= (ahead_of_rest if d == farthest(side) else 0)) & (t < units))
                         def _():
-                            hop(d, i - lag(d, side), side).start()
+                            hop(d, t, side).start()
 
             if shared:
                 @pl.loop(shared, units - 1)
@@ -583,6 +616,7 @@
     shared = units * 10 // 16 if cols > 3 and grps == 2 else 0
     places = units + shared + 1
     blocks = row_dev // BLOCK
+    chunks = half // max(own, LANES)
     table, w = tables(rows, row_dev, half)
     dma = pltpu.SemaphoreType.DMA
     flow = pltpu.VMEM((cols, units, UNIT, row_dev), jnp.float32)
@@ -595,7 +629,8 @@
         out_specs=pl.BlockSpec(memory_space=pltpu.VMEM),
         scratch_shapes=[
             pltpu.VMEM((depth, half), lwe_matrix.dtype),
-            pltpu.VMEM((half, depth), lwe_matrix.dtype),
+            pltpu.VMEM((min(2, chunks) * half // chunks, depth), lwe_matrix.dtype),
+            pltpu.VMEM((max(chunks - 2, 1) * half // chunks, depth), lwe_matrix.dtype),
             pltpu.VMEM((blocks, BLOCK, depth), database.dtype),
             flow,
             flow,
@@ -610,10 +645,10 @@
             pltpu.VMEM((cols, 8, row_dev // 4), jnp.float32),
             pltpu.VMEM((2, 8, row_dev // 4), jnp.float32),
             dma((3,)),
-            dma((4,)),
-            dma((blocks,)),
+            dma((chunks,)),
+            dma((AHEAD,)),
             dma((2, cols)),
-            dma((cols + 1, units)),
+            dma((cols if shared and cols == 4 else cols + 1, units)),
             dma((max(rows - 1, 1),)),
             dma((max(rows - 1, 1), places)),
             dma((1,)),

time: 74.5 us -> 73.7 us (0.989)
    pallas_call x1, Pallas kernels: 73.7 us -> 73 us  [body(): pl.pallas_call(functools.partial(kernel, cols, rows, grps, shared), out_s...]
where the time goes in v7:
time: 73.7 us; the launch traced here: 73.6 us
  Pallas kernels  73 us (99%)
    pallas_call x1, Pallas kernels, body(): pl.pallas_call(functools.partial(kernel, cols, rows, grps, shared), out_s...  73 us

profile of v7, /device:TPU:0, one launch (start us, length us, event | category | flops | bytes accessed | tf_op | source)
XLA Modules:
  0.0 73.6 jit_solution(13067487915057929380)
XLA Ops:
  0.0 73.0 %shard_map.55 = f32[2,2,2048]{2,1,0:T(2,128)S(1)} custom-call(bf16[2048,512]{1,0:T(8,128)(2,1)} %bitcast.3, bf16[2048,2048]{1,0:T(8,128)(2,1)} %d_hbm.1, f32[2,2,16,8,2048]{4,3,2,1,0:T(8,128)} %bitcast.2, f32[2,6,16,128]{3,2,1,0:T(8,128)} %constant.4.clone.table_hbm, bf16[768,256]{1,0:T(8,128)(2,1)} %constant.5.clone.w_hbm), custom_call_target="tpu_custom_call" | custom-call | tf_op jit(solution)/shard_map/pallas_call | solution.py:625
  73.0 0.6 copy.7

commit v8 on v7

--- a/solution.py
+++ b/solution.py
@@ -15,6 +15,8 @@
 BLOCK = 256
 LEAD = 4
 AHEAD = 4
+HEAD = 5
+PAIR = 2
 EARLY = 4
 NEXT = 2
 DELAY = 4
@@ -79,6 +81,7 @@
     end = first | last
     beside = jnp.where(first, 1, cols - 2)
     giver = ((me == 1) | (me == cols - 2)) if shared else None
+    head = max(min(HEAD, shared), shared - units // 2)
     late = units - shared if shared else 0
     right_hold = HOLD * jnp.maximum(me - 1, 0)
     left_hold = HOLD * jnp.maximum(cols - 2 - me, 0)
@@ -154,6 +157,8 @@
         )
 
     early, ahead_of_rest = min(EARLY, units), min(EARLY + NEXT, units)
+    couple = units // recv_sem.shape[1]
+    starts = lambda t: lax.rem(t, couple) == 0
     farthest = lambda side: cols - 1 if side > 0 else 0
 
     def early_hop(b, side):
@@ -167,10 +172,10 @@
 
     def hop(d, t, side, to=None):
         landing, lane = (from_left, 0) if side > 0 else (from_right, 1)
-        src, dst = part.at[d, t], landing.at[d, t]
+        src, dst = part.at[d, pl.ds(t, couple)], landing.at[d, pl.ds(t, couple)]
         to = me + side if to is None else to
         slot = d if side > 0 or recv_sem.shape[0] == cols else jnp.where(d == to, cols, d)
-        return remote(src, dst, send_sem.at[lane, d], recv_sem.at[slot, t], {"col": me + side})
+        return remote(src, dst, send_sem.at[lane, d], recv_sem.at[slot, t // couple], {"col": me + side})
 
     def arrived(d, t, side):
         hop(d, t, side, to=me).wait_recv()
@@ -214,7 +219,7 @@
     if shared:
         @pl.when(giver)
         def _():
-            @pl.loop(0, shared)
+            @pl.loop(0, head)
             def _(u):
                 give(u).start()
 
@@ -252,7 +257,7 @@
                 for there, side in ((first, 1), (last, -1)):
                     @pl.when(there)
                     def _():
-                        for t in range(early, ahead_of_rest):
+                        for t in range(early, ahead_of_rest, couple):
                             hop(farthest(side), t, side).start()
 
             loads[-1].start()
@@ -289,7 +294,7 @@
                     if d != near(side):
                         t = i - lag(d, side)
 
-                        @pl.when((t >= (ahead_of_rest if d == farthest(side) else 0)) & (t < units))
+                        @pl.when((t >= (ahead_of_rest if d == farthest(side) else 0)) & (t < units) & starts(t))
                         def _():
                             hop(d, t, side).start()
 
@@ -337,7 +342,10 @@
     late_from = jnp.maximum(units + LEAD, shared + own_hold)
 
     def place(i):
-        at_end = jnp.where(i < shared, units + i, i - shared)
+        k = i - head
+        group, r = k // 3, lax.rem(k, 3)
+        mixed = jnp.where(r == 2, units + head + group, 2 * group + r)
+        at_end = jnp.where(k < 0, units + i, jnp.where(group < shared - head, mixed, i - shared))
         m = i - late_from
         inside = jnp.where(m < 0, i - own_hold, shared + m)
         if late > 1:
@@ -368,10 +376,12 @@
         )
         t = i - hold - lag(d, side)
 
-        @pl.when(jnp.logical_not(end) & beyond & (t >= (early if d == farthest(side) else 0)) & (t < units))
+        first_one = early if d == farthest(side) else 0
+
+        @pl.when(jnp.logical_not(end) & beyond & (t >= first_one) & (t < units) & starts(t))
         def _():
             arrived(d, t, side)
-            part[d, t] += landing[d, t]
+            part[d, pl.ds(t, couple)] += landing[d, pl.ds(t, couple)]
             hop(d, t, side).start()
 
     def step_of(i, carry):
@@ -379,6 +389,13 @@
             forward(d, 1, i)
         for d in range(cols - 2):
             forward(d, -1, i)
+        if shared > head:
+            g = i - HOLD * (cols - 3) - 1
+
+            @pl.when(giver & (g >= 0) & (g < 2 * (shared - head)) & (lax.rem(g, 2) == 0))
+            def _():
+                give(head + g // 2).start()
+
         busy, u = place(i)
 
         if shared:
@@ -413,21 +430,27 @@
                         def _(b):
                             early_hop(b, side).wait_recv()
 
-            by_blocks = end & (t < early)
+            awaited, lead = starts(t), t
+            if late > 1 and couple > 1:
+                awaited = jnp.where(
+                    jnp.logical_not(end) & (t >= units - 2), t == units - 1, awaited
+                )
+                lead = t - lax.rem(t, couple)
+            awaited = awaited & jnp.logical_not(end & (t < early))
 
             @pl.when(whole_left & jnp.logical_not(lent))
             def _():
-                @pl.when(jnp.logical_not(by_blocks))
+                @pl.when(awaited)
                 def _():
-                    arrived(me, t, 1)
+                    arrived(me, lead, 1)
 
                 part[me, t] += from_left[me, t]
 
             @pl.when(whole_right & jnp.logical_not(lent))
             def _():
-                @pl.when(jnp.logical_not(by_blocks))
+                @pl.when(awaited)
                 def _():
-                    arrived(me, t, -1)
+                    arrived(me, lead, -1)
 
                 part[me, t] += from_right[me, t]
 
@@ -617,6 +640,7 @@
     places = units + shared + 1
     blocks = row_dev // BLOCK
     chunks = half // max(own, LANES)
+    couple = PAIR if units % PAIR == 0 and EARLY % PAIR == 0 and NEXT % PAIR == 0 else 1
     table, w = tables(rows, row_dev, half)
     dma = pltpu.SemaphoreType.DMA
     flow = pltpu.VMEM((cols, units, UNIT, row_dev), jnp.float32)
@@ -648,7 +672,7 @@
             dma((chunks,)),
             dma((AHEAD,)),
             dma((2, cols)),
-            dma((cols if shared and cols == 4 else cols + 1, units)),
+            dma((cols if shared and cols == 4 else cols + 1, units // couple)),
             dma((max(rows - 1, 1),)),
             dma((max(rows - 1, 1), places)),
             dma((1,)),

time: 73.7 us -> 72.2 us (0.980)
  Pallas kernels: 73 us -> 71.5 us
    pallas_call x1, Pallas kernels: 73 us -> 71.5 us  [body(): pl.pallas_call(functools.partial(kernel, cols, rows, grps, shared), out_s...]
where the time goes in v8:
time: 72.2 us; the launch traced here: 72.1 us
  Pallas kernels  71.5 us (99%)
    pallas_call x1, Pallas kernels, body(): pl.pallas_call(functools.partial(kernel, cols, rows, grps, shared), out_s...  71.5 us

profile of v8, /device:TPU:0, one launch (start us, length us, event | category | flops | bytes accessed | tf_op | source)
XLA Modules:
  0.0 72.1 jit_solution(9145925215225911142)
XLA Ops:
  0.0 71.5 %shard_map.55 = f32[2,2,2048]{2,1,0:T(2,128)S(1)} custom-call(bf16[2048,512]{1,0:T(8,128)(2,1)} %bitcast.3, bf16[2048,2048]{1,0:T(8,128)(2,1)} %d_hbm.1, f32[2,2,16,8,2048]{4,3,2,1,0:T(8,128)} %bitcast.2, f32[2,6,16,128]{3,2,1,0:T(8,128)} %constant.4.clone.table_hbm, bf16[768,256]{1,0:T(8,128)(2,1)} %constant.5.clone.w_hbm), custom_call_target="tpu_custom_call" | custom-call | tf_op jit(solution)/shard_map/pallas_call | solution.py:649
  71.5 0.6 copy.7

commit v9 on v8

--- a/solution.py
+++ b/solution.py
@@ -20,7 +20,7 @@
 EARLY = 4
 NEXT = 2
 DELAY = 4
-PIECES = 1
+PIECES = 2
 LAG = 3
 END_LAG = 5
 HOLD = 3
@@ -339,7 +339,7 @@
                 acc[k, 1, :, lanes] += r * b + i * a
 
     extra = jnp.where(giver, 1, 0) if shared else 0
-    late_from = jnp.maximum(units + LEAD, shared + own_hold)
+    late_from = jnp.maximum(units + LEAD - 2, shared + own_hold)
 
     def place(i):
         k = i - head

time: 72.2 us -> 71.6 us (level)
  no operation moved by 1% of the time
where the time goes in v9:
time: 71.6 us; the launch traced here: 71.5 us
  Pallas kernels  70.9 us (99%)
    pallas_call x1, Pallas kernels, body(): pl.pallas_call(functools.partial(kernel, cols, rows, grps, shared), out_s...  70.9 us

profile of v9, /device:TPU:0, one launch (start us, length us, event | category | flops | bytes accessed | tf_op | source)
XLA Modules:
  0.0 71.5 jit_solution(11392472514013804015)
XLA Ops:
  0.0 70.9 %shard_map.55 = f32[2,2,2048]{2,1,0:T(2,128)S(1)} custom-call(bf16[2048,512]{1,0:T(8,128)(2,1)} %bitcast.3, bf16[2048,2048]{1,0:T(8,128)(2,1)} %d_hbm.1, f32[2,2,16,8,2048]{4,3,2,1,0:T(8,128)} %bitcast.2, f32[2,6,16,128]{3,2,1,0:T(8,128)} %constant.4.clone.table_hbm, bf16[768,256]{1,0:T(8,128)(2,1)} %constant.5.clone.w_hbm), custom_call_target="tpu_custom_call" | custom-call | tf_op jit(solution)/shard_map/pallas_call | solution.py:649
  70.9 0.6 copy.7

commit v10 on v9

--- a/solution.py
+++ b/solution.py
@@ -13,12 +13,12 @@
 UNIT = 8
 LANES = 128
 BLOCK = 256
-LEAD = 4
+LEAD = 6
 AHEAD = 4
 HEAD = 5
 PAIR = 2
-EARLY = 4
-NEXT = 2
+EARLY = 6
+NEXT = 0
 DELAY = 4
 PIECES = 2
 LAG = 3
@@ -70,7 +70,7 @@
 def kernel(cols, rows, grps, shared, l_hbm, d_hbm, s_hbm, table_hbm, w_hbm, out_ref,
            l_buf, lt_outer, lt_inner, d_buf, part, from_left, from_right, land, cipher, table, w, acc,
            half_sum, half_in, z_in, whole_sum,
-           load_sem, l_sem, d_sem, send_sem, recv_sem, row_send, row_recv, s_send, s_recv, y_send, y_recv,
+           load_sem, l_sem, d_sem, send_sem, recv_sem, row_send, row_recv, s_send, y_send,
            limb_send, limb_recv, z_send, z_recv, near_send, near_recv, bit_recv, pair_send, pair_recv, early_recv):
     me, row = lax.axis_index("col"), lax.axis_index("row")
     grp, limb = lax.axis_index("grp"), lax.axis_index("limb")
@@ -209,12 +209,12 @@
     def give(u):
         there = jnp.where(me == 1, 0, cols - 1)
         return remote(
-            s_hbm.at[grp, :, u], cipher.at[grp, :, units + u], s_send.at[0], s_recv.at[u], {"col": there}
+            s_hbm.at[grp, :, u], cipher.at[grp, :, units + u], s_send.at[0], near_recv.at[u // PIECES, lax.rem(u, PIECES)], {"col": there}
         )
 
     def swap(u):
         here = cipher.at[grp, :, units + u]
-        return remote(here, here, y_send.at[0], y_recv.at[u], {"grp": 1 - grp})
+        return remote(here, here, y_send.at[0], bit_recv.at[0, u // PIECES, lax.rem(u, PIECES)], {"grp": 1 - grp})
 
     if shared:
         @pl.when(giver)
@@ -644,7 +644,7 @@
     table, w = tables(rows, row_dev, half)
     dma = pltpu.SemaphoreType.DMA
     flow = pltpu.VMEM((cols, units, UNIT, row_dev), jnp.float32)
-    lots = max(shared, 1)
+    tail = max(units - 1 - shared, -(-shared // PIECES), 1)
     hbm = pl.BlockSpec(memory_space=pl.ANY)
     return pl.pallas_call(
         functools.partial(kernel, cols, rows, grps, shared),
@@ -676,16 +676,14 @@
             dma((max(rows - 1, 1),)),
             dma((max(rows - 1, 1), places)),
             dma((1,)),
-            dma((lots,)),
             dma((1,)),
-            dma((lots,)),
             dma((2,)),
             dma((2,)),
             dma((1,)),
             dma((cols,)),
             dma((1,)),
-            dma((max(units - 1 - shared, 1), PIECES)),
-            dma((max(rows - 1, 1), max(units - 1 - shared, 1), PIECES)),
+            dma((tail, PIECES)),
+            dma((max(rows - 1, 1), tail, PIECES)),
             dma((1,)),
             dma((rows,)),
             dma((2, blocks)),

time: 71.6 us -> 71.4 us (level)
  no operation moved by 1% of the time
where the time goes in v10:
time: 71.4 us; the launch traced here: 71.3 us
  Pallas kernels  70.6 us (99%)
    pallas_call x1, Pallas kernels, body(): pl.pallas_call(functools.partial(kernel, cols, rows, grps, shared), out_s...  70.6 us

profile of v10, /device:TPU:0, one launch (start us, length us, event | category | flops | bytes accessed | tf_op | source)
XLA Modules:
  0.0 71.3 jit_solution(10881944449932327486)
XLA Ops:
  0.0 70.6 %shard_map.55 = f32[2,2,2048]{2,1,0:T(2,128)S(1)} custom-call(bf16[2048,512]{1,0:T(8,128)(2,1)} %bitcast.3, bf16[2048,2048]{1,0:T(8,128)(2,1)} %d_hbm.1, f32[2,2,16,8,2048]{4,3,2,1,0:T(8,128)} %bitcast.2, f32[2,6,16,128]{3,2,1,0:T(8,128)} %constant.4.clone.table_hbm, bf16[768,256]{1,0:T(8,128)(2,1)} %constant.5.clone.w_hbm), custom_call_target="tpu_custom_call" | custom-call | tf_op jit(solution)/shard_map/pallas_call | solution.py:649
  70.6 0.6 copy.7
